TPU v7x, 32 devices: a whole 2x2x4 slice. The times are simulated.
32 devices in a mesh: batch: 4 (over y, x), heads: 8 (over z, core).
Axes of the slice: x: 2, y: 2, z: 4, core: 2. Of those that a mesh axis runs over, the one named last changes fastest.
Arguments:
- tokens: bfloat16 [2, 1024, 4, 2048], P(None, 'heads', 'batch'), may hold values from -6 to 6
- out_grad: bfloat16 [2, 1024, 4, 2048], P(None, 'heads', 'batch'), may hold values from -6 to 6
- row_seq: int32 [2, 4], P(None, 'batch'), may hold values from 0 to 7, as said below
- seq_lengths: int32 [8], replicated, may hold values from 384 to 1024, as said below
- norm1_gain: float32 [2048], P(('batch', 'heads')), may hold values from 0.5 to 1.5
- norm1_bias: float32 [2048], P(('batch', 'heads')), may hold values from -1.25 to 1.25
- qkv_weight: bfloat16 [2048, 3, 2048], P(None, None, 'heads'), may hold values from -0.125 to 0.125
- qk_bias: bfloat16 [2, 32, 64], P(None, 'heads'), may hold values from -3 to 3
- v_bias: bfloat16 [32, 64], P('heads'), may hold values from -0.25 to 0.25
- out_weight: bfloat16 [2048, 2048], P('heads'), may hold values from -0.75 to 0.75
- norm2_gain: float32 [2048], P(('batch', 'heads')), may hold values from 0.5 to 1.5
- norm2_bias: float32 [2048], P(('batch', 'heads')), may hold values from -1.25 to 1.25
- gate_weight: bfloat16 [2048, 5632], P('batch', 'heads'), may hold values from -0.125 to 0.125
- up_weight: bfloat16 [2048, 5632], P('batch', 'heads'), may hold values from -0.125 to 0.125
- down_weight: bfloat16 [2048, 5632], P('batch', 'heads'), may hold values from -0.078125 to 0.078125
Outputs:
- layer_out: bfloat16 [2, 1024, 4, 2048], P(None, 'heads', 'batch')
- input_grad: bfloat16 [2, 1024, 4, 2048], P(None, 'heads', 'batch')
- norm1_gain_grad: float32 [2048], P(('batch', 'heads'))
- norm1_bias_grad: float32 [2048], P(('batch', 'heads'))
- qkv_weight_grad: float32 [2048, 3, 2048], P('batch', None, 'heads')
- qk_bias_grad: float32 [2, 32, 64], P(None, 'heads', 'batch')
- v_bias_grad: float32 [32, 64], P('heads', 'batch')
- out_weight_grad: float32 [2048, 2048], P('heads', 'batch')
- norm2_gain_grad: float32 [2048], P(('batch', 'heads'))
- norm2_bias_grad: float32 [2048], P(('batch', 'heads'))
- gate_weight_grad: float32 [2048, 5632], P('batch', 'heads')
- up_weight_grad: float32 [2048, 5632], P('batch', 'heads')
- down_weight_grad: float32 [2048, 5632], P('batch', 'heads')
Inputs may be any that keep to these rules, and one draw needn't show every extreme that they name: `seq_lengths`: each index of batch holds 2 rows over all micro-batches; one of them holds a sequence of exactly 1024 tokens. `row_seq`: every sequence number is held by exactly one row.
All inputs are finite; a program needn't handle non-finite values.
Results may differ from a plain program's by a relative error of at most 0.024.
Values may be sent and summed in bfloat16 or wider, within the bound.
No kernel may reach another device: no remote copies, remote signals or barrier semaphores. Data moves between devices by JAX's collectives and lax.ppermute only.
A program may use at most 192 MiB of HBM per device.

v0:
```python
import jax
import jax.numpy as jnp
from jax import lax
from jax.sharding import PartitionSpec as P

HD = 64
ROT = 16


eps = 1e-05
neg_big = -1e30
rope_base = 10000.0


def row_norm(values, gain_vec, shift_vec):
    average = jnp.mean(values, axis=-1, keepdims=True)
    centred = values - average
    inverse = lax.rsqrt(jnp.mean(centred * centred, axis=-1, keepdims=True) + eps)
    unit_rows = centred * inverse
    return (unit_rows * gain_vec + shift_vec, unit_rows, inverse)


def norm_back(gradient, unit_rows, inverse, gain_vec):
    scaled_grad = gradient * gain_vec
    return inverse * (
        scaled_grad
        - jnp.mean(scaled_grad, axis=-1, keepdims=True)
        - unit_rows * jnp.mean(scaled_grad * unit_rows, axis=-1, keepdims=True)
    )


def rope_tables(length_all):
    half_rot = ROT // 2
    frequency = rope_base ** (-(2.0 * jnp.arange(half_rot, dtype=jnp.float32)) / ROT)
    angles = jnp.arange(length_all, dtype=jnp.float32)[:, None] * frequency[None, :]
    return (jnp.cos(angles)[:, None, None, :], jnp.sin(angles)[:, None, None, :])


def rotate(values, cosine, sine):
    half_rot = ROT // 2
    first_half = values[..., :half_rot]
    second_half = values[..., half_rot:ROT]
    return jnp.concatenate(
        [
            first_half * cosine - second_half * sine,
            second_half * cosine + first_half * sine,
            values[..., ROT:],
        ],
        axis=-1,
    )


def rotate_back(gradient, cosine, sine):
    half_rot = ROT // 2
    first_half = gradient[..., :half_rot]
    second_half = gradient[..., half_rot:ROT]
    return jnp.concatenate(
        [
            first_half * cosine + second_half * sine,
            second_half * cosine - first_half * sine,
            gradient[..., ROT:],
        ],
        axis=-1,
    )


def block_scores(query_block, keys, start, key_index, block, length, scale):
    key_block = lax.dynamic_slice_in_dim(keys, key_index * block, block, 0)
    scores = (
        jnp.einsum("qhd,khd->hqk", query_block, key_block, preferred_element_type=jnp.float32)
        * scale
    )
    query_pos = start + jnp.arange(block, dtype=jnp.int32)
    key_pos = key_index * block + jnp.arange(block, dtype=jnp.int32)
    keep = (key_pos[None, :] <= query_pos[:, None]) & (key_pos[None, :] < length)
    return jnp.where(keep[None], scores, neg_big)


def attend_row(query, keys, values, length):
    seq_all, heads_here, size_head = query.shape
    block = min(512, seq_all)
    count_blocks = seq_all // block
    scale = size_head ** (-0.5)

    def one_block(block_index):
        start = block_index * block
        query_block = lax.dynamic_slice_in_dim(query, start, block, 0)
        reach = jnp.maximum(1, jnp.minimum(block_index + 1, (length + block - 1) // block))

        def stats(key_index, carry):
            row_top, row_total = carry
            scores = block_scores(query_block, keys, start, key_index, block, length, scale)
            new_top = jnp.maximum(row_top, jnp.max(scores, axis=-1))
            row_total = row_total * jnp.exp(row_top - new_top) + jnp.sum(
                jnp.exp(scores - new_top[..., None]), axis=-1
            )
            return (new_top, row_total)

        start_top = jnp.full((heads_here, block), neg_big, jnp.float32)
        row_top, row_total = lax.fori_loop(
            0, reach, stats, (start_top, jnp.zeros((heads_here, block), jnp.float32))
        )
        log_total = row_top + jnp.log(row_total)

        def gather_values(key_index, accum):
            scores = block_scores(query_block, keys, start, key_index, block, length, scale)
            weights = jnp.exp(scores - log_total[..., None]).astype(jnp.bfloat16)
            value_block = lax.dynamic_slice_in_dim(values, key_index * block, block, 0)
            return accum + jnp.einsum(
                "hqk,khd->qhd", weights, value_block, preferred_element_type=jnp.float32
            )

        result = lax.fori_loop(
            0, reach, gather_values, jnp.zeros((block, heads_here, size_head), jnp.float32)
        )
        return (result, log_total)

    results, log_totals = lax.map(one_block, jnp.arange(count_blocks, dtype=jnp.int32))
    return (results.reshape(seq_all, heads_here, size_head), log_totals)


def attend_back(query, keys, values, log_totals, grad_mixed, offsets, length):
    seq_all, heads_here, size_head = query.shape
    block = min(512, seq_all)
    count_blocks = seq_all // block
    scale = size_head ** (-0.5)

    def one_block(block_index, carry):
        grad_q, grad_k, grad_v = carry
        start = block_index * block
        query_block = lax.dynamic_slice_in_dim(query, start, block, 0)
        grad_block = lax.dynamic_slice_in_dim(grad_mixed, start, block, 0)
        log_total = log_totals[block_index]
        offset = offsets[block_index]
        reach = jnp.maximum(1, jnp.minimum(block_index + 1, (length + block - 1) // block))

        def inner_step(key_index, state):
            accum, keys_grad, values_grad = state
            scores = block_scores(query_block, keys, start, key_index, block, length, scale)
            weights = jnp.exp(scores - log_total[..., None])
            key_start = key_index * block
            key_block = lax.dynamic_slice_in_dim(keys, key_start, block, 0)
            value_block = lax.dynamic_slice_in_dim(values, key_start, block, 0)
            grad_weights = jnp.einsum(
                "qhd,khd->hqk", grad_block, value_block, preferred_element_type=jnp.float32
            )
            grad_scores = (weights * (grad_weights - offset[..., None])).astype(jnp.bfloat16)
            accum = (
                accum
                + jnp.einsum(
                    "hqk,khd->qhd", grad_scores, key_block, preferred_element_type=jnp.float32
                )
                * scale
            )
            key_piece = (
                jnp.einsum(
                    "hqk,qhd->khd", grad_scores, query_block, preferred_element_type=jnp.float32
                )
                * scale
            )
            value_piece = jnp.einsum(
                "hqk,qhd->khd",
                weights.astype(jnp.bfloat16),
                grad_block,
                preferred_element_type=jnp.float32,
            )
            keys_grad = lax.dynamic_update_slice_in_dim(
                keys_grad,
                lax.dynamic_slice_in_dim(keys_grad, key_start, block, 0) + key_piece,
                key_start,
                0,
            )
            values_grad = lax.dynamic_update_slice_in_dim(
                values_grad,
                lax.dynamic_slice_in_dim(values_grad, key_start, block, 0) + value_piece,
                key_start,
                0,
            )
            return (accum, keys_grad, values_grad)

        start_accum = jnp.zeros((block, heads_here, size_head), jnp.float32)
        accum, grad_k, grad_v = lax.fori_loop(0, reach, inner_step, (start_accum, grad_k, grad_v))
        grad_q = lax.dynamic_update_slice_in_dim(grad_q, accum, start, 0)
        return (grad_q, grad_k, grad_v)

    zero_grads = jnp.zeros(query.shape, jnp.float32)
    return lax.fori_loop(0, count_blocks, one_block, (zero_grads, zero_grads, zero_grads))


def run_forward(row_item):
    return attend_row(row_item[0], row_item[1], row_item[2], row_item[3])


def run_backward(row_item):
    return attend_back(
        row_item[0], row_item[1], row_item[2], row_item[3], row_item[4], row_item[5], row_item[6]
    )


def by_row(values):
    return jnp.moveaxis(values, 1, 0)


def local(
    tokens,
    out_grad,
    row_seq,
    seq_lengths,
    norm1_gain,
    norm1_bias,
    qkv_weight,
    qk_bias,
    v_bias,
    out_weight,
    norm2_gain,
    norm2_bias,
    gate_weight,
    up_weight,
    down_weight,
):
    gain_one, shift_one, gain_two, shift_two = (
        lax.all_gather(norm1_gain, ("batch", "heads"), axis=0, tiled=True),
        lax.all_gather(norm1_bias, ("batch", "heads"), axis=0, tiled=True),
        lax.all_gather(norm2_gain, ("batch", "heads"), axis=0, tiled=True),
        lax.all_gather(norm2_bias, ("batch", "heads"), axis=0, tiled=True),
    )
    seq_here = tokens.shape[1]
    rows_here = tokens.shape[2]
    seq_full = seq_here * lax.axis_size("heads")
    width_here = qkv_weight.shape[2]
    heads_here = width_here // HD
    block = min(512, seq_full)
    count_blocks = seq_full // block
    table = jnp.arange(seq_lengths.shape[0], dtype=jnp.int32)
    row_len = jnp.sum(jnp.where(row_seq[..., None] == table, seq_lengths, 0), axis=-1)
    positions = lax.axis_index("heads") * seq_here + jnp.arange(seq_here, dtype=jnp.int32)
    cosine, sine = rope_tables(seq_full)
    bias_query = qk_bias[0].reshape(width_here).astype(jnp.float32)
    bias_keys = qk_bias[1].reshape(width_here).astype(jnp.float32)
    bias_values = v_bias.reshape(width_here).astype(jnp.float32)
    shape_heads = (seq_full, rows_here, heads_here, HD)

    def gather_mlp():
        return (
            lax.all_gather(gate_weight, "batch", axis=0, tiled=True),
            lax.all_gather(up_weight, "batch", axis=0, tiled=True),
            lax.all_gather(down_weight, "batch", axis=0, tiled=True),
        )

    sum_proj = jnp.zeros(qkv_weight.shape, jnp.float32)
    sum_out = jnp.zeros(out_weight.shape, jnp.float32)
    sum_bias = jnp.zeros((3, width_here), jnp.float32)
    sum_gate = jnp.zeros(
        (gate_weight.shape[0] * lax.axis_size("batch"), gate_weight.shape[1]), jnp.float32
    )
    sum_up = jnp.zeros(sum_gate.shape, jnp.float32)
    sum_down = jnp.zeros(sum_gate.shape, jnp.float32)
    sum_gain_one = jnp.zeros(gain_one.shape, jnp.float32)
    sum_shift_one = jnp.zeros(gain_one.shape, jnp.float32)
    sum_gain_two = jnp.zeros(gain_one.shape, jnp.float32)
    sum_shift_two = jnp.zeros(gain_one.shape, jnp.float32)
    outputs = []
    input_grads = []
    for batch_index in range(tokens.shape[0]):
        length = row_len[batch_index]
        valid = (positions[:, None] < length[None, :]).astype(jnp.float32)[..., None]
        inputs = tokens[batch_index].astype(jnp.float32)
        normed_one, unit_one, inverse_one = row_norm(inputs, gain_one, shift_one)
        normed_all = lax.all_gather(normed_one.astype(jnp.bfloat16), "heads", axis=0, tiled=True)
        projected = jnp.einsum(
            "srd,dcj->srcj", normed_all, qkv_weight, preferred_element_type=jnp.float32
        )
        query = rotate((projected[:, :, 0] + bias_query).reshape(shape_heads), cosine, sine).astype(
            jnp.bfloat16
        )
        keys = rotate((projected[:, :, 1] + bias_keys).reshape(shape_heads), cosine, sine).astype(
            jnp.bfloat16
        )
        values = (projected[:, :, 2] + bias_values).reshape(shape_heads).astype(jnp.bfloat16)
        mixed_rows, log_totals = lax.map(
            run_forward, (by_row(query), by_row(keys), by_row(values), length)
        )
        mixed = jnp.moveaxis(mixed_rows, 0, 1)
        mixed_low = mixed.reshape(seq_full, rows_here, width_here).astype(jnp.bfloat16)
        branch = lax.psum_scatter(
            jnp.einsum(
                "srj,jd->srd", mixed_low, out_weight, preferred_element_type=jnp.float32
            ).astype(jnp.bfloat16),
            "heads",
            scatter_dimension=0,
            tiled=True,
        ).astype(jnp.float32)
        state = inputs + branch
        normed_two, unit_two, inverse_two = row_norm(state, gain_two, shift_two)
        mlp_all_in = lax.all_gather(normed_two.astype(jnp.bfloat16), "heads", axis=0, tiled=True)
        gate_full, up_full, down_full = gather_mlp()
        gate_value = jnp.einsum(
            "srd,df->srf", mlp_all_in, gate_full, preferred_element_type=jnp.float32
        )
        up_value = jnp.einsum(
            "srd,df->srf", mlp_all_in, up_full, preferred_element_type=jnp.float32
        )
        sigma = jax.nn.sigmoid(gate_value)
        silu_value = gate_value * sigma
        inner = (silu_value * up_value).astype(jnp.bfloat16)
        mlp_part = lax.psum_scatter(
            jnp.einsum("srf,df->srd", inner, down_full, preferred_element_type=jnp.float32).astype(
                jnp.bfloat16
            ),
            "heads",
            scatter_dimension=0,
            tiled=True,
        ).astype(jnp.float32)
        outputs.append(((state + mlp_part) * valid).astype(jnp.bfloat16))
        grad_y = out_grad[batch_index].astype(jnp.float32) * valid
        grad_all = lax.all_gather(grad_y.astype(jnp.bfloat16), "heads", axis=0, tiled=True)
        gate_back, up_back, down_back = gather_mlp()
        grad_inner = jnp.einsum(
            "srd,df->srf", grad_all, down_back, preferred_element_type=jnp.float32
        )
        grad_gate = (grad_inner * up_value * sigma * (1.0 + gate_value * (1.0 - sigma))).astype(
            jnp.bfloat16
        )
        grad_up = (grad_inner * silu_value).astype(jnp.bfloat16)
        sum_down = sum_down + jnp.einsum(
            "srd,srf->df", grad_all, inner, preferred_element_type=jnp.float32
        )
        sum_gate = sum_gate + jnp.einsum(
            "srd,srf->df", mlp_all_in, grad_gate, preferred_element_type=jnp.float32
        )
        sum_up = sum_up + jnp.einsum(
            "srd,srf->df", mlp_all_in, grad_up, preferred_element_type=jnp.float32
        )
        grad_normed_two = lax.psum_scatter(
            (
                jnp.einsum("srf,df->srd", grad_gate, gate_back, preferred_element_type=jnp.float32)
                + jnp.einsum("srf,df->srd", grad_up, up_back, preferred_element_type=jnp.float32)
            ).astype(jnp.bfloat16),
            "heads",
            scatter_dimension=0,
            tiled=True,
        ).astype(jnp.float32)
        sum_gain_two = sum_gain_two + jnp.sum(grad_normed_two * unit_two, axis=(0, 1))
        sum_shift_two = sum_shift_two + jnp.sum(grad_normed_two, axis=(0, 1))
        grad_state = grad_y + norm_back(grad_normed_two, unit_two, inverse_two, gain_two)
        grad_state_all = lax.all_gather(
            grad_state.astype(jnp.bfloat16), "heads", axis=0, tiled=True
        )
        sum_out = sum_out + jnp.einsum(
            "srj,srd->jd", mixed_low, grad_state_all, preferred_element_type=jnp.float32
        )
        grad_mixed = (
            jnp.einsum(
                "srd,jd->srj", grad_state_all, out_weight, preferred_element_type=jnp.float32
            )
            .astype(jnp.bfloat16)
            .reshape(shape_heads)
        )
        offsets = jnp.sum(grad_mixed.astype(jnp.float32) * mixed, axis=-1)
        offset_rows = (
            jnp.moveaxis(offsets, 1, 0)
            .reshape(rows_here, count_blocks, block, heads_here)
            .transpose(0, 1, 3, 2)
        )
        grad_q, grad_k, grad_v = lax.map(
            run_backward,
            (
                by_row(query),
                by_row(keys),
                by_row(values),
                log_totals,
                by_row(grad_mixed),
                offset_rows,
                length,
            ),
        )
        grad_q = rotate_back(jnp.moveaxis(grad_q, 0, 1), cosine, sine).reshape(
            seq_full, rows_here, width_here
        )
        grad_k = rotate_back(jnp.moveaxis(grad_k, 0, 1), cosine, sine).reshape(
            seq_full, rows_here, width_here
        )
        grad_v = jnp.moveaxis(grad_v, 0, 1).reshape(seq_full, rows_here, width_here)
        grad_proj = jnp.stack([grad_q, grad_k, grad_v], axis=2).astype(jnp.bfloat16)
        sum_proj = sum_proj + jnp.einsum(
            "srd,srcj->dcj", normed_all, grad_proj, preferred_element_type=jnp.float32
        )
        sum_bias = sum_bias + jnp.sum(grad_proj.astype(jnp.float32), axis=(0, 1))
        grad_normed_one = lax.psum_scatter(
            jnp.einsum(
                "srcj,dcj->srd", grad_proj, qkv_weight, preferred_element_type=jnp.float32
            ).astype(jnp.bfloat16),
            "heads",
            scatter_dimension=0,
            tiled=True,
        ).astype(jnp.float32)
        sum_gain_one = sum_gain_one + jnp.sum(grad_normed_one * unit_one, axis=(0, 1))
        sum_shift_one = sum_shift_one + jnp.sum(grad_normed_one, axis=(0, 1))
        input_grads.append(
            (grad_state + norm_back(grad_normed_one, unit_one, inverse_one, gain_one)).astype(
                jnp.bfloat16
            )
        )
    bias_qk_sum = sum_bias[:2].reshape(2, heads_here, HD)
    bias_v_sum = sum_bias[2].reshape(heads_here, HD)
    summed = (
        lax.psum_scatter(
            sum_proj.astype(jnp.bfloat16), "batch", scatter_dimension=0, tiled=True
        ).astype(jnp.float32),
        lax.psum_scatter(
            sum_out.astype(jnp.bfloat16), "batch", scatter_dimension=1, tiled=True
        ).astype(jnp.float32),
        lax.psum_scatter(
            bias_qk_sum.astype(jnp.bfloat16), "batch", scatter_dimension=2, tiled=True
        ).astype(jnp.float32),
        lax.psum_scatter(
            bias_v_sum.astype(jnp.bfloat16), "batch", scatter_dimension=1, tiled=True
        ).astype(jnp.float32),
        lax.psum_scatter(
            sum_gate.astype(jnp.bfloat16), "batch", scatter_dimension=0, tiled=True
        ).astype(jnp.float32),
        lax.psum_scatter(
            sum_up.astype(jnp.bfloat16), "batch", scatter_dimension=0, tiled=True
        ).astype(jnp.float32),
        lax.psum_scatter(
            sum_down.astype(jnp.bfloat16), "batch", scatter_dimension=0, tiled=True
        ).astype(jnp.float32),
    )
    norm_sums = (
        lax.psum_scatter(sum_gain_one, ("batch", "heads"), scatter_dimension=0, tiled=True),
        lax.psum_scatter(sum_shift_one, ("batch", "heads"), scatter_dimension=0, tiled=True),
        lax.psum_scatter(sum_gain_two, ("batch", "heads"), scatter_dimension=0, tiled=True),
        lax.psum_scatter(sum_shift_two, ("batch", "heads"), scatter_dimension=0, tiled=True),
    )
    return (
        jnp.stack(outputs),
        jnp.stack(input_grads),
        norm_sums[0],
        norm_sums[1],
        summed[0],
        summed[2],
        summed[3],
        summed[1],
        norm_sums[2],
        norm_sums[3],
        summed[4],
        summed[5],
        summed[6],
    )


def solution(mesh):
    placed = (
        P(None, "heads", "batch", None),
        P(None, "heads", "batch", None),
        P(None, "batch"),
        P(),
        P(("batch", "heads")),
        P(("batch", "heads")),
        P(None, None, "heads"),
        P(None, "heads", None),
        P("heads", None),
        P("heads", None),
        P(("batch", "heads")),
        P(("batch", "heads")),
        P("batch", "heads"),
        P("batch", "heads"),
        P("batch", "heads"),
    )
    return jax.shard_map(
        local,
        mesh=mesh,
        in_specs=placed,
        out_specs=(
            P(None, "heads", "batch", None),
            P(None, "heads", "batch", None),
            P(("batch", "heads")),
            P(("batch", "heads")),
            P("batch", None, "heads"),
            P(None, "heads", "batch"),
            P("heads", "batch"),
            P("heads", "batch"),
            P(("batch", "heads")),
            P(("batch", "heads")),
            P("batch", "heads"),
            P("batch", "heads"),
            P("batch", "heads"),
        ),
        check_vma=False,
    )
```

profile of v0, /device:TPU:0, one launch (start us, length us, event | category | flops | bytes accessed | tf_op | source)
XLA Modules:
  0.0 1286.9 jit_solution(2575213495623537623)
XLA Ops:
  14.5 42.2 %all-reduce.11 = (f32[2048]{0:T(1024)}, f32[2048]{0:T(1024)}, f32[2048]{0:T(1024)S(1)}, f32[2048]{0:T(1024)S(1)}) all-reduce(f32[2048]{0:T(1024)S(1)} %dynamic-update-slice.3, f32[2048]{0:T(1024)S(1)} %dynamic-update-slice.2, f32[2048]{0:T(1024)S(1)} %dynamic-update-slice.1, ...), channel_id=1, replica_groups=mesh['batch'=4,'heads'=8] {'batch','heads'}, use_global_device_ids=true, to_apply=%add.3 | all-reduce | flops 8192 | bytes 65536
  60.8 46.0 %all-gather.12.cloned.1.call-done = bf16[1024,1,2048]{2,0,1:T(8,128)(2,1)} async-done(((bf16[128,1,2048]{2,0,1:T(8,128)(2,1)}), bf16[1024,1,2048]{2,0,1:T(8,128)(2,1)}) %all-gather.12.cloned.1.call-update) | async-done | bytes 4194320 | tf_op jit(solution)/shard_map/all_gather | solution.py:269
  116.5 29.7 %while.276 = (s32[]{:T(128)}, f32[2,512,4,64]{1,3,2,0:T(8,128)}, f32[2,4,512]{2,1,0:T(4,128)S(1)}, s32[2]{0:T(128)S(1)}, s32[]{:T(128)}, /*index=5*/bf16[1024,4,...) while((s32[]{:T(128)}, f32[2,512,4,64]{1,3,2,0:T(8,128)}, ...), condition=%wide.region_10.11_spmd, body=%wide.region_3.10_spmd.sunk | while | flops 415377408 | bytes 14340497 | solution.py:118
  152.7 57.0 %reduce-scatter.16.cloned.1.call-done = bf16[128,1,2048]{2,0,1:T(8,128)(2,1)} async-done(((bf16[1024,1,2048]{2,0,1:T(8,128)(2,1)}), bf16[128,1,2048]{2,0,1:T(8,128)(2,1)}) %reduce-scatter.16.cloned.1.call-update) | async-done | bytes 524304 | tf_op jit(solution)/shard_map/reduce_scatter | solution.py:285
  214.4 44.7 %all-gather.22.cloned.1.call-done = bf16[1024,1,2048]{2,0,1:T(8,128)(2,1)} async-done(((bf16[128,1,2048]{2,0,1:T(8,128)(2,1)}), bf16[1024,1,2048]{2,0,1:T(8,128)(2,1)}) %all-gather.22.cloned.1.call-update) | async-done | bytes 4194320 | tf_op jit(solution)/shard_map/all_gather | solution.py:269
  268.8 38.2 %while.279 = (s32[]{:T(128)}, f32[2,512,4,64]{1,3,2,0:T(8,128)}, f32[2,4,512]{2,1,0:T(4,128)S(1)}, s32[2]{0:T(128)S(1)}, s32[]{:T(128)}, /*index=5*/bf16[1024,4,...) while((s32[]{:T(128)}, f32[2,512,4,64]{1,3,2,0:T(8,128)}, ...), condition=%wide.region_24.25_spmd, body=%wide.region_17.24_spmd.sunk | while | flops 415377408 | bytes 14340497 | solution.py:118
  313.9 47.3 %reduce-scatter.20.cloned.1.call-done = bf16[128,1,2048]{2,0,1:T(8,128)(2,1)} async-done(((bf16[1024,1,2048]{2,0,1:T(8,128)(2,1)}), bf16[128,1,2048]{2,0,1:T(8,128)(2,1)}) %reduce-scatter.20.cloned.1.call-update) | async-done | bytes 524304 | tf_op jit(solution)/shard_map/reduce_scatter | solution.py:285
  372.8 11.9 reduce-scatter.28.cloned.1.call-start
  384.8 26.6 %all-gather.24.cloned.1.call-done = bf16[1024,1,2048]{2,0,1:T(8,128)(2,1)} async-done(((bf16[128,1,2048]{2,0,1:T(8,128)(2,1)}), bf16[1024,1,2048]{2,0,1:T(8,128)(2,1)}) %all-gather.24.cloned.1.call-update) | async-done | bytes 4194320 | tf_op jit(solution)/shard_map/all_gather | solution.py:295
  419.3 34.1 %all-gather.16.cloned.1.call-done = bf16[2048,704]{0,1:T(8,128)(2,1)} async-done(((bf16[512,704]{0,1:T(8,128)(2,1)}), bf16[2048,704]{0,1:T(8,128)(2,1)}) %all-gather.16.cloned.1.call-update) | async-done | bytes 2883600 | tf_op jit(solution)/shard_map/all_gather | solution.py:245
  461.2 35.6 %all-gather.20.cloned.1.call-done = bf16[2048,704]{0,1:T(8,128)(2,1)} async-done(((bf16[512,704]{0,1:T(8,128)(2,1)}), bf16[2048,704]{0,1:T(8,128)(2,1)}) %all-gather.20.cloned.1.call-update) | async-done | bytes 2883600 | tf_op jit(solution)/shard_map/all_gather | solution.py:247
  496.8 49.0 %all-gather.30.cloned.1.call-done = bf16[1024,1,2048]{2,0,1:T(8,128)(2,1)} async-done(((bf16[128,1,2048]{2,0,1:T(8,128)(2,1)}), bf16[1024,1,2048]{2,0,1:T(8,128)(2,1)}) %all-gather.30.cloned.1.call-update) | async-done | bytes 4194320 | tf_op jit(solution)/shard_map/all_gather | solution.py:316
  545.8 10.1 multiply_convert_fusion
  573.2 27.2 %all-gather.14.cloned.1.call-done = bf16[1024,1,2048]{2,0,1:T(8,128)(2,1)} async-done(((bf16[128,1,2048]{2,0,1:T(8,128)(2,1)}), bf16[1024,1,2048]{2,0,1:T(8,128)(2,1)}) %all-gather.14.cloned.1.call-update) | async-done | bytes 4194320 | tf_op jit(solution)/shard_map/all_gather | solution.py:295
  613.1 49.5 %all-gather.26.cloned.1.call-done = bf16[1024,1,2048]{2,0,1:T(8,128)(2,1)} async-done(((bf16[128,1,2048]{2,0,1:T(8,128)(2,1)}), bf16[1024,1,2048]{2,0,1:T(8,128)(2,1)}) %all-gather.26.cloned.1.call-update) | async-done | bytes 4194320 | tf_op jit(solution)/shard_map/all_gather | solution.py:316
  662.6 10.2 multiply_convert_fusion.2
  690.0 27.2 %reduce-scatter.22.cloned.1.call-done = bf16[128,1,2048]{2,0,1:T(8,128)(2,1)} async-done(((bf16[1024,1,2048]{2,0,1:T(8,128)(2,1)}), bf16[128,1,2048]{2,0,1:T(8,128)(2,1)}) %reduce-scatter.22.cloned.1.call-update) | async-done | bytes 524304 | tf_op jit(solution)/shard_map/reduce_scatter | solution.py:306
  717.1 50.5 %reduce-scatter.24.cloned.1.call-done = bf16[128,1,2048]{2,0,1:T(8,128)(2,1)} async-done(((bf16[1024,1,2048]{2,0,1:T(8,128)(2,1)}), bf16[128,1,2048]{2,0,1:T(8,128)(2,1)}) %reduce-scatter.24.cloned.1.call-update) | async-done | bytes 524304 | tf_op jit(solution)/shard_map/reduce_scatter | solution.py:334
  767.6 50.5 %reduce-scatter.18.cloned.1.call-done = bf16[128,1,2048]{2,0,1:T(8,128)(2,1)} async-done(((bf16[1024,1,2048]{2,0,1:T(8,128)(2,1)}), bf16[128,1,2048]{2,0,1:T(8,128)(2,1)}) %reduce-scatter.18.cloned.1.call-update) | async-done | bytes 524304 | tf_op jit(solution)/shard_map/reduce_scatter | solution.py:306
  857.5 13.5 %all-gather.32.cloned.1.call-done = bf16[1024,1,2048]{2,0,1:T(8,128)(2,1)} async-done(((bf16[128,1,2048]{2,0,1:T(8,128)(2,1)}), bf16[1024,1,2048]{2,0,1:T(8,128)(2,1)}) %all-gather.32.cloned.1.call-update) | async-done | bytes 4194320 | tf_op jit(solution)/shard_map/all_gather | solution.py:346
  884.0 39.3 %while.283 = (s32[]{:T(128)}, f32[1024,4,64]{0,2,1:T(8,128)}, f32[1024,4,64]{0,2,1:T(8,128)}, f32[1024,4,64]{0,2,1:T(8,128)}, s32[]{:T(128)}, /*index=5*/bf16[10...) while((s32[]{:T(128)}, f32[1024,4,64]{0,2,1:T(8,128)}, ...), condition=%wide.region_47.48_spmd, body=%wide.region_44.47_spmd.sunk | while | flops 682756096 | bytes 45156180 | solution.py:187
  887.0 10.0 while.289
  901.5 19.9 %while.289 = (s32[]{:T(128)}, f32[512,4,64]{0,2,1:T(8,128)}, f32[1024,4,64]{0,2,1:T(8,128)}, f32[1024,4,64]{0,2,1:T(8,128)}, s32[]{:T(128)}, /*index=5*/bf16[102...) while((s32[]{:T(128)}, f32[512,4,64]{0,2,1:T(8,128)}, ...), condition=%wide.region_46.46_spmd, body=%wide.region_45.45_spmd.sunk | while | flops 682756096 | bytes 42501556 | solution.py:182
  936.1 29.2 %while.281 = (s32[]{:T(128)}, f32[1024,4,64]{0,2,1:T(8,128)}, f32[1024,4,64]{0,2,1:T(8,128)}, f32[1024,4,64]{0,2,1:T(8,128)}, s32[]{:T(128)}, /*index=5*/bf16[10...) while((s32[]{:T(128)}, f32[1024,4,64]{0,2,1:T(8,128)}, ...), condition=%wide.region_36.37_spmd, body=%wide.region_33.36_spmd.sunk | while | flops 682756096 | bytes 45156180 | solution.py:187
  938.8 10.0 while.288
  953.3 10.0 while.288
  1033.8 17.0 %reduce-scatter.40.cloned.1.call-done = bf16[512,704]{0,1:T(8,128)(2,1)} async-done(((bf16[2048,704]{0,1:T(8,128)(2,1)}), bf16[512,704]{0,1:T(8,128)(2,1)}) %reduce-scatter.40.cloned.1.call-update) | async-done | bytes 720912 | tf_op jit(solution)/shard_map/reduce_scatter | solution.py:425
  1067.1 14.8 %reduce-scatter.34.cloned.1.call-done = bf16[256,512]{1,0:T(8,128)(2,1)} async-done(((bf16[256,2048]{1,0:T(8,128)(2,1)}), bf16[256,512]{1,0:T(8,128)(2,1)}) %reduce-scatter.34.cloned.1.call-update) | async-done | bytes 262160 | tf_op jit(solution)/shard_map/reduce_scatter | solution.py:410
  1083.7 45.3 %reduce-scatter.32.cloned.1.call-done = bf16[512,3,256]{2,0,1:T(8,128)(2,1)} async-done(((bf16[2048,3,256]{2,0,1:T(8,128)(2,1)}), bf16[512,3,256]{2,0,1:T(8,128)(2,1)}) %reduce-scatter.32.cloned.1.call-update) | async-done | bytes 786448 | tf_op jit(solution)/shard_map/reduce_scatter | solution.py:407
  1131.5 49.8 %reduce-scatter.30.cloned.1.call-done = bf16[128,1,2048]{2,0,1:T(8,128)(2,1)} async-done(((bf16[1024,1,2048]{2,0,1:T(8,128)(2,1)}), bf16[128,1,2048]{2,0,1:T(8,128)(2,1)}) %reduce-scatter.30.cloned.1.call-update) | async-done | bytes 524304 | tf_op jit(solution)/shard_map/reduce_scatter | solution.py:389
  1181.3 50.4 %reduce-scatter.26.cloned.1.call-done = bf16[128,1,2048]{2,0,1:T(8,128)(2,1)} async-done(((bf16[1024,1,2048]{2,0,1:T(8,128)(2,1)}), bf16[128,1,2048]{2,0,1:T(8,128)(2,1)}) %reduce-scatter.26.cloned.1.call-update) | async-done | bytes 524304 | tf_op jit(solution)/shard_map/reduce_scatter | solution.py:389
  1234.4 38.2 %all-reduce.10 = (f32[2048]{0:T(1024)S(1)}, f32[2048]{0:T(1024)S(1)}, f32[2048]{0:T(1024)S(1)}, f32[2048]{0:T(1024)S(1)}) all-reduce(f32[2048]{0:T(1024)S(1)} %add.792, f32[2048]{0:T(1024)S(1)} %add.793, f32[2048]{0:T(1024)S(1)} %add.797, f32[2048]{0:T(1024)S(1)} %add.798), channel_id=10, replica_groups=mesh['batch'=4,'heads'=8] {'batch','heads'}, use_global_device_ids=true, to_apply=%region_53.54.clone | all-reduce | flops 8192 | bytes 65536
  (574 shorter events, 454.2 us)
Async XLA Ops:
  8.1 98.7 %all-gather.12.cloned.1.call-start = ((), (), s32[]{:S(2)}) async-start(), calls=%async_computation.13 | async-start | bytes 4718592 | tf_op jit(solution)/shard_map/all_gather | solution.py:269
  56.7 154.7 %copy-start.47 = (f32[2048]{0:T(1024)}, f32[2048]{0:T(1024)S(1)}, u32[]{:S(2)}) copy-start(f32[2048]{0:T(1024)S(1)} %get-tuple-element.1876) | copy-start | bytes 24580
  59.0 150.7 %reduce-scatter.16.cloned.1.call-start = ((), (), s32[]{:S(2)}) async-start(), calls=%async_computation.14 | async-start | bytes 4718592 | tf_op jit(solution)/shard_map/reduce_scatter | solution.py:285
  60.8 204.2 %copy-start.39 = (f32[1024,8]{0,1:T(8,128)}, f32[1024,8]{0,1:T(8,128)S(1)}, u32[]{:S(2)}) copy-start(f32[1024,8]{0,1:T(8,128)S(1)} %get-tuple-element.1961) | copy-start | bytes 98308
  60.8 204.2 %copy-start.41 = (f32[1024,8]{0,1:T(8,128)}, f32[1024,8]{0,1:T(8,128)S(1)}, u32[]{:S(2)}) copy-start(f32[1024,8]{0,1:T(8,128)S(1)} %get-tuple-element.1962) | copy-start | bytes 98308
  152.3 106.8 %all-gather.22.cloned.1.call-start = ((), (), s32[]{:S(2)}) async-start(), calls=%async_computation.20 | async-start | bytes 4718592 | tf_op jit(solution)/shard_map/all_gather | solution.py:269
  213.7 147.5 %reduce-scatter.20.cloned.1.call-start = ((), (), s32[]{:S(2)}) async-start(), calls=%async_computation.21 | async-start | bytes 4718592 | tf_op jit(solution)/shard_map/reduce_scatter | solution.py:285
  313.2 71.5 %all-gather.18.cloned.1.call-start = ((), (), s32[]{:S(2)}) async-start(), calls=%async_computation.17 | async-start | bytes 3604480 | tf_op jit(solution)/shard_map/all_gather | solution.py:246
  313.8 97.6 %all-gather.24.cloned.1.call-start = ((), (), s32[]{:S(2)}) async-start(), calls=%async_computation.22 | async-start | bytes 4718592 | tf_op jit(solution)/shard_map/all_gather | solution.py:295
  366.4 87.1 %all-gather.16.cloned.1.call-start = ((), (), s32[]{:S(2)}) async-start(), calls=%async_computation.16 | async-start | bytes 3604480 | tf_op jit(solution)/shard_map/all_gather | solution.py:245
  367.0 129.9 %all-gather.20.cloned.1.call-start = ((), (), s32[]{:S(2)}) async-start(), calls=%async_computation.18 | async-start | bytes 3604480 | tf_op jit(solution)/shard_map/all_gather | solution.py:247
  367.7 178.1 %all-gather.30.cloned.1.call-start = ((), (), s32[]{:S(2)}) async-start(), calls=%async_computation.28 | async-start | bytes 4718592 | tf_op jit(solution)/shard_map/all_gather | solution.py:316
  371.5 228.9 %all-gather.14.cloned.1.call-start = ((), (), s32[]{:S(2)}) async-start(), calls=%async_computation.15 | async-start | bytes 4718592 | tf_op jit(solution)/shard_map/all_gather | solution.py:295
  372.2 290.4 %all-gather.26.cloned.1.call-start = ((), (), s32[]{:S(2)}) async-start(), calls=%async_computation.24 | async-start | bytes 4718592 | tf_op jit(solution)/shard_map/all_gather | solution.py:316
  372.8 317.1 %reduce-scatter.28.cloned.1.call-start = ((), (), s32[]{:S(2)}) async-start(), calls=%async_computation.29 | async-start | bytes 4718592 | tf_op jit(solution)/shard_map/reduce_scatter | solution.py:334
  565.0 152.1 %reduce-scatter.22.cloned.1.call-start = ((), (), s32[]{:S(2)}) async-start(), calls=%async_computation.23 | async-start | bytes 4718592 | tf_op jit(solution)/shard_map/reduce_scatter | solution.py:306
  572.8 194.8 %reduce-scatter.24.cloned.1.call-start = ((), (), s32[]{:S(2)}) async-start(), calls=%async_computation.25 | async-start | bytes 4718592 | tf_op jit(solution)/shard_map/reduce_scatter | solution.py:334
  682.0 136.0 %reduce-scatter.18.cloned.1.call-start = ((), (), s32[]{:S(2)}) async-start(), calls=%async_computation.19 | async-start | bytes 4718592 | tf_op jit(solution)/shard_map/reduce_scatter | solution.py:306
  689.9 181.1 %all-gather.32.cloned.1.call-start = ((), (), s32[]{:S(2)}) async-start(), calls=%async_computation.30 | async-start | bytes 4718592 | tf_op jit(solution)/shard_map/all_gather | solution.py:346
  826.0 97.3 %all-gather.28.cloned.1.call-start = ((), (), s32[]{:S(2)}) async-start(), calls=%async_computation.26 | async-start | bytes 4718592 | tf_op jit(solution)/shard_map/all_gather | solution.py:346
  826.6 202.5 %reduce-scatter.38.cloned.1.call-start = ((), (), s32[]{:S(2)}) async-start(), calls=%async_computation.35 | async-start | bytes 3604480 | tf_op jit(solution)/shard_map/reduce_scatter | solution.py:422
  836.7 194.7 %reduce-scatter.36.cloned.1.call-start = ((), (), s32[]{:S(2)}) async-start(), calls=%async_computation.34 | async-start | bytes 3604480 | tf_op jit(solution)/shard_map/reduce_scatter | solution.py:419
  847.2 203.7 %reduce-scatter.40.cloned.1.call-start = ((), (), s32[]{:S(2)}) async-start(), calls=%async_computation.36 | async-start | bytes 3604480 | tf_op jit(solution)/shard_map/reduce_scatter | solution.py:425
  857.4 224.5 %reduce-scatter.34.cloned.1.call-start = ((), (), s32[]{:S(2)}) async-start(), calls=%async_computation.33 | async-start | bytes 1310720 | tf_op jit(solution)/shard_map/reduce_scatter | solution.py:410
  979.5 149.6 %reduce-scatter.32.cloned.1.call-start = ((), (), s32[]{:S(2)}) async-start(), calls=%async_computation.32 | async-start | bytes 3932160 | tf_op jit(solution)/shard_map/reduce_scatter | solution.py:407
  1013.8 167.4 %reduce-scatter.30.cloned.1.call-start = ((), (), s32[]{:S(2)}) async-start(), calls=%async_computation.31 | async-start | bytes 4718592 | tf_op jit(solution)/shard_map/reduce_scatter | solution.py:389
  1020.4 211.4 %reduce-scatter.26.cloned.1.call-start = ((), (), s32[]{:S(2)}) async-start(), calls=%async_computation.27 | async-start | bytes 4718592 | tf_op jit(solution)/shard_map/reduce_scatter | solution.py:389
  1055.8 176.0 %copy-start.48 = (f32[2048]{0:T(1024)S(1)}, f32[2048]{0:T(1024)}, u32[]{:S(2)}) copy-start(f32[2048]{0:T(1024)} %copy-done.47) | copy-start | bytes 24580
  1055.8 176.0 %copy-start.56 = (f32[128]{0:T(128)S(1)}, f32[128]{0:T(128)}, u32[]{:S(2)}) copy-start(f32[128]{0:T(128)} %copy-done.55) | copy-start | bytes 1540
  1055.8 176.0 %copy-start.58 = (f32[128]{0:T(128)S(1)}, f32[128]{0:T(128)}, u32[]{:S(2)}) copy-start(f32[128]{0:T(128)} %copy-done.57) | copy-start | bytes 1540
  1055.8 176.0 %copy-start.60 = (f32[128]{0:T(128)S(1)}, f32[128]{0:T(128)}, u32[]{:S(2)}) copy-start(f32[128]{0:T(128)} %copy-done.59) | copy-start | bytes 1540
  1055.8 176.0 %copy-start.62 = (f32[128]{0:T(128)S(1)}, f32[128]{0:T(128)}, u32[]{:S(2)}) copy-start(f32[128]{0:T(128)} %copy-done.61) | copy-start | bytes 1540
  (100 other events, 1188.7 us)
Sparse Core Ops, SparseCore 0:
  59.1 47.6 all-gather.11
  152.4 57.1 reduce-scatter.15
  213.8 45.2 all-gather.21
  313.3 47.7 reduce-scatter.19
  565.1 98.7 reduce-scatter.27
  666.0 51.0 reduce-scatter.21
  719.4 48.1 reduce-scatter.23
  769.9 48.1 reduce-scatter.17
Sparse Core Ops, SparseCore 1:
  315.5 39.3 all-gather.17
  366.5 44.9 all-gather.23
  413.1 40.3 all-gather.15
  455.3 41.5 all-gather.19
  499.0 46.7 all-gather.29
  548.0 52.3 all-gather.13
  602.4 60.1 all-gather.25
  826.1 44.9 all-gather.31
  872.5 45.5 all-gather.27
  921.1 40.4 reduce-scatter.37
  964.5 41.6 reduce-scatter.35
  1009.2 41.6 reduce-scatter.39
  1054.2 27.7 reduce-scatter.33
  1085.2 43.8 reduce-scatter.31
  1131.5 49.8 reduce-scatter.29
  1183.7 48.0 reduce-scatter.25
where the time goes:
time: 1300 us; the launch traced here: 1290 us
  waiting for transfers between devices  740 us (57%)
  matrix products  234 us (18%)
  other arithmetic  92.2 us (7%)
  local copies, waits for them, and re-layouts  91.6 us (7%)
  blocking collectives  89.6 us (7%)
  between operations  19.4 us (1%)
  starting transfers between devices  13.5 us (1%)
    reduce_scatter x2, waiting for transfers between devices, local(): lax.psum_scatter(jnp.einsum('srj,jd->srd', mixed_low, out_weight, preferr...  104 us
    reduce_scatter x2, waiting for transfers between devices, local(): lax.psum_scatter(jnp.einsum('srcj,dcj->srd', grad_proj, qkv_weight, prefe...  100 us
    all_gather x2, waiting for transfers between devices, local(): lax.all_gather(grad_y.astype(jnp.bfloat16), 'heads', axis=0, tiled=True)  98.5 us
    all_gather x2, waiting for transfers between devices, local(): lax.all_gather(normed_one.astype(jnp.bfloat16), 'heads', axis=0, tiled=True)  90.7 us
    unnamed x3, blocking collectives  89.6 us
    reduce_scatter x2, waiting for transfers between devices, local(): lax.psum_scatter(jnp.einsum('srf,df->srd', inner, down_full, preferred_el...  77.6 us
    all_gather x2, waiting for transfers between devices, local(): lax.all_gather(normed_two.astype(jnp.bfloat16), 'heads', axis=0, tiled=True)  53.8 us
    reduce_scatter x2, waiting for transfers between devices, local(): lax.psum_scatter((jnp.einsum('srf,df->srd', grad_gate, gate_back, preferr...  50.5 us
  transfers between devices with their start and end apart: 24, of which 19 were waited for; matrix products, arithmetic and copies ran while one was open for 22% of the time, Pallas kernels for 0%

commit v1 on v0

v1 whole, which is shorter than its diff:
```python
import functools
import math

import jax
import jax.numpy as jnp
from jax import lax
from jax.experimental import pallas as pl
from jax.experimental.pallas import tpu as pltpu
from jax.sharding import PartitionSpec as P

HD = 64
ROT = 16
EPS = 1e-05
NEG = -1e30
ROPE_BASE = 10000.0
SCALE = HD ** (-0.5)
LOG2E = math.log2(math.e)
F32 = jnp.float32
BF16 = jnp.bfloat16


def dot(a, b, ca, cb):
    return lax.dot_general(a, b, (((ca,), (cb,)), ((), ())), preferred_element_type=F32)


def row_norm(values, gain_vec, shift_vec):
    average = jnp.mean(values, axis=-1, keepdims=True)
    centred = values - average
    inverse = lax.rsqrt(jnp.mean(centred * centred, axis=-1, keepdims=True) + EPS)
    unit_rows = centred * inverse
    return (unit_rows * gain_vec + shift_vec, unit_rows, inverse)


def norm_back(gradient, unit_rows, inverse, gain_vec):
    scaled_grad = gradient * gain_vec
    return inverse * (
        scaled_grad
        - jnp.mean(scaled_grad, axis=-1, keepdims=True)
        - unit_rows * jnp.mean(scaled_grad * unit_rows, axis=-1, keepdims=True)
    )


class Line:
    def __init__(self):
        self.devices = lax.axis_size("heads")
        self.chips = self.devices // 2
        index = lax.axis_index("heads")
        self.chip = index // 2
        self.core = index % 2

    def hop(self, value, sources, step):
        pairs = [(2 * i + c, 2 * (i + step) + c) for i in sources for c in range(2)]
        return lax.ppermute(value, "heads", pairs)

    def swap(self, value):
        pairs = [(2 * i + c, 2 * i + 1 - c) for i in range(self.chips) for c in range(2)]
        return lax.ppermute(value, "heads", pairs)

    def gather(self, block):
        n = self.chips
        ups, downs = [block], [block]
        for step in range(1, n):
            ups.append(self.hop(ups[-1], range(step - 1, n - 1), 1))
            downs.append(self.hop(downs[-1], range(1, n - step + 1), -1))
        pieces = [block]
        for k in range(1, n):
            pieces.append(jnp.where(self.chip >= k, ups[k], downs[n - k]))
        return jnp.concatenate(pieces, axis=0)

    def scatter(self, pieces):
        n = self.chips
        up = down = None
        for m in range(n - 1, 0, -1):
            value_up = pieces[n - m] if up is None else add_low(pieces[n - m], up)
            value_down = pieces[m] if down is None else add_low(pieces[m], down)
            up = self.hop(value_up, range(0, n - m), 1)
            down = self.hop(value_down, range(m, n), -1)
        return pieces[0].astype(F32) + up.astype(F32) + down.astype(F32)


def after(value, *earlier):
    return lax.optimization_barrier((value, *earlier))[0]


def add_low(a, b):
    return (a.astype(F32) + b.astype(F32)).astype(BF16)


def shifts(value_of, axis):
    n = lax.axis_size(axis)
    received = [value_of(0)]
    for k in range(1, n):
        received.append(lax.ppermute(value_of(k), axis, [(i, (i + k) % n) for i in range(n)]))
    return received


def small_gather(value, axis):
    n = lax.axis_size(axis)
    received = shifts(lambda k: value, axis)
    width = value.shape[1]
    ordered = jnp.concatenate(received[::-1], axis=1)
    doubled = jnp.concatenate([ordered, ordered], axis=1)
    start = (n - 1 - lax.axis_index(axis)) * width
    return lax.dynamic_slice_in_dim(doubled, start, n * width, 1)


def small_scatter(value, axis, dim):
    n = lax.axis_size(axis)
    width = value.shape[dim] // n
    me = lax.axis_index(axis)

    def part(k):
        return lax.dynamic_slice_in_dim(value, ((me + k) % n) * width, width, dim)

    return functools.reduce(jnp.add, shifts(part, axis))


def piece_rows(where_ref, s, k, chips, size):
    chip, core = where_ref[0], where_ref[1]
    owner = lax.rem(chip - k + chips, chips)
    other = core if s == 0 else 1 - core
    return pl.multiple_of((2 * owner + other) * size, size)


def head_mask(shape, head):
    lane = lax.broadcasted_iota(jnp.int32, shape, len(shape) - 1)
    return (lane >= head * HD) & (lane < (head + 1) * HD)


def keep_mask(size, start, length):
    key = lax.broadcasted_iota(jnp.int32, (size, size), 0)
    query = lax.broadcasted_iota(jnp.int32, (size, size), 1)
    return (key <= query) & (key + start < length)


def turn(x, cos, plus, minus):
    half = ROT // 2
    width = x.shape[1]
    return x * cos + pltpu.roll(x, half, 1) * plus + pltpu.roll(x, width - half, 1) * minus


def forward_kernel(
    chips, heads, where_ref, own_ref, sib_ref, bias_ref, cos_ref, plus_ref, minus_ref,
    attn_own_ref, attn_sib_ref, qkv_ref, lse_ref, vt_ref, s_ref, attn_ref,
):
    width = heads * HD
    rows = qkv_ref.shape[0]
    size = rows // (2 * chips)
    block = min(256, rows)
    length = where_ref[2]
    for s, half in enumerate((own_ref, sib_ref)):
        for k in range(chips):
            at = pl.ds(piece_rows(where_ref, s, k, chips, size), size)
            raw = half[k * size : (k + 1) * size, :] + bias_ref[...]
            cos, plus, minus = cos_ref[at, :], plus_ref[at, :], minus_ref[at, :]
            for part in range(2):
                x = raw[:, part * width : (part + 1) * width]
                qkv_ref[at, part * width : (part + 1) * width] = turn(x, cos, plus, minus).astype(BF16)
            qkv_ref[at, 2 * width :] = raw[:, 2 * width :].astype(BF16)
    vt_ref[...] = jnp.transpose(qkv_ref[:, 2 * width :])
    for i in range(rows // block):
        here = slice(i * block, (i + 1) * block)
        reach = (i + 1) * block

        @pl.when(i * block < length)
        def _():
            query = qkv_ref[here, :width]
            keys = qkv_ref[:reach, width : 2 * width]
            keep = keep_mask(block, i * block, length)
            pieces = []
            for head in range(heads):
                masked = jnp.where(head_mask(query.shape, head), query, jnp.zeros_like(query))
                s_ref[:reach, :] = dot(keys, masked, 1, 1)
                s_ref[here, :] = jnp.where(keep, s_ref[here, :], NEG)
                scores = s_ref[:reach, :] * (SCALE * LOG2E)
                top = jnp.max(scores, axis=0, keepdims=True)
                weights = jnp.exp2(scores - top)
                total = jnp.sum(weights, axis=0, keepdims=True)
                low = weights.astype(BF16)
                mixed = dot(vt_ref[head * HD : (head + 1) * HD, :reach], low, 1, 0)
                pieces.append(mixed * (1.0 / total))
                lse_ref[head : head + 1, here] = top + jnp.log2(total)
            attn_ref[here, :] = jnp.transpose(jnp.concatenate(pieces, axis=0)).astype(BF16)

        @pl.when(i * block >= length)
        def _():
            attn_ref[here, :] = jnp.zeros((block, width), BF16)
            lse_ref[:, here] = jnp.zeros((lse_ref.shape[0], block), F32)

    for s, half in enumerate((attn_own_ref, attn_sib_ref)):
        for k in range(chips):
            at = pl.ds(piece_rows(where_ref, s, k, chips, size), size)
            half[k * size : (k + 1) * size, :] = attn_ref[at, :]


def backward_kernel(
    chips, heads, where_ref, own_ref, sib_ref, qkv_ref, lse_ref, cos_ref, plus_ref, minus_ref,
    grad_own_ref, grad_sib_ref, bias_grad_ref,
    g_ref, kt_ref, qs_ref, gs_ref, p_ref, d_ref, pcat_ref, scat_ref, dq_ref, dk_ref, dv_ref,
):
    width = heads * HD
    rows = qkv_ref.shape[0]
    size = rows // (2 * chips)
    block = min(256, rows)
    length = where_ref[2]
    for s, half in enumerate((own_ref, sib_ref)):
        for k in range(chips):
            at = pl.ds(piece_rows(where_ref, s, k, chips, size), size)
            g_ref[at, :] = half[k * size : (k + 1) * size, :]
    kt_ref[...] = jnp.transpose(qkv_ref[:, width : 2 * width])
    dk_ref[...] = jnp.zeros_like(dk_ref)
    dv_ref[...] = jnp.zeros_like(dv_ref)
    for i in range(rows // block):
        here = slice(i * block, (i + 1) * block)
        reach = (i + 1) * block

        @pl.when(i * block < length)
        def _():
            query = qkv_ref[here, :width]
            grad = g_ref[here, :]
            keys = qkv_ref[:reach, width : 2 * width]
            values = qkv_ref[:reach, 2 * width :]
            keep = keep_mask(block, i * block, length)
            pieces = []
            for head in range(heads):
                mask = head_mask(query.shape, head)
                cols = slice(head * block, (head + 1) * block)
                qs_ref[cols, :] = jnp.where(mask, query, jnp.zeros_like(query))
                gs_ref[cols, :] = jnp.where(mask, grad, jnp.zeros_like(grad))
                p_ref[:reach, :] = dot(keys, qs_ref[cols, :], 1, 1)
                p_ref[here, :] = jnp.where(keep, p_ref[here, :], NEG)
                weights = jnp.exp2(p_ref[:reach, :] * (SCALE * LOG2E) - lse_ref[head : head + 1, here])
                pcat_ref[:reach, cols] = weights.astype(BF16)
                p_ref[:reach, :] = weights
                d_ref[:reach, :] = dot(values, gs_ref[cols, :], 1, 1)
                offset = jnp.sum(p_ref[:reach, :] * d_ref[:reach, :], axis=0, keepdims=True)
                low = (p_ref[:reach, :] * (d_ref[:reach, :] - offset)).astype(BF16)
                scat_ref[:reach, cols] = low
                pieces.append(dot(kt_ref[head * HD : (head + 1) * HD, :reach], low, 1, 0))
            dv_ref[:reach, :] += dot(pcat_ref[:reach, :], gs_ref[...], 1, 0)
            dk_ref[:reach, :] += dot(scat_ref[:reach, :], qs_ref[...], 1, 0)
            dq_ref[here, :] = jnp.transpose(jnp.concatenate(pieces, axis=0))

        @pl.when(i * block >= length)
        def _():
            dq_ref[here, :] = jnp.zeros((block, width), F32)

    sums = [jnp.zeros((1, width), F32) for _ in range(3)]
    for s, half in enumerate((grad_own_ref, grad_sib_ref)):
        for k in range(chips):
            at = pl.ds(piece_rows(where_ref, s, k, chips, size), size)
            to = slice(k * size, (k + 1) * size)
            cos, plus, minus = cos_ref[at, :], plus_ref[at, :], minus_ref[at, :]
            parts = (
                turn(dq_ref[at, :] * SCALE, cos, -plus, -minus),
                turn(dk_ref[at, :] * SCALE, cos, -plus, -minus),
                dv_ref[at, :],
            )
            for j, part in enumerate(parts):
                low = part.astype(BF16)
                half[to, j * width : (j + 1) * width] = low
                sums[j] = sums[j] + jnp.sum(low.astype(F32), axis=0, keepdims=True)
    bias_grad_ref[...] = jnp.concatenate([jnp.broadcast_to(x, (8, width)) for x in sums], axis=1)


VMEM = pl.BlockSpec(memory_space=pltpu.VMEM)
SMEM = pl.BlockSpec(memory_space=pltpu.SMEM)


def attend(where, own, sib, bias, tables, chips, heads):
    width = heads * HD
    rows = 2 * own.shape[0]
    block = min(256, rows)
    return pl.pallas_call(
        functools.partial(forward_kernel, chips, heads),
        out_shape=(
            jax.ShapeDtypeStruct((rows // 2, width), BF16),
            jax.ShapeDtypeStruct((rows // 2, width), BF16),
            jax.ShapeDtypeStruct((rows, 3 * width), BF16),
            jax.ShapeDtypeStruct((8, rows), F32),
        ),
        in_specs=[SMEM] + [VMEM] * 6,
        out_specs=[VMEM] * 4,
        scratch_shapes=[
            pltpu.VMEM((width, rows), BF16),
            pltpu.VMEM((rows, block), F32),
            pltpu.VMEM((rows, width), BF16),
        ],
        compiler_params=pltpu.CompilerParams(vmem_limit_bytes=32 << 20),
        cost_estimate=pl.CostEstimate(
            flops=heads * rows * rows * 512, transcendentals=heads * rows * rows // 2, bytes_accessed=8 << 20
        ),
        name="attend",
    )(where, own, sib, bias, *tables)


def attend_back(where, own, sib, qkv, lse, tables, chips, heads):
    width = heads * HD
    rows = 2 * own.shape[0]
    block = min(256, rows)
    return pl.pallas_call(
        functools.partial(backward_kernel, chips, heads),
        out_shape=(
            jax.ShapeDtypeStruct((rows // 2, 3 * width), BF16),
            jax.ShapeDtypeStruct((rows // 2, 3 * width), BF16),
            jax.ShapeDtypeStruct((8, 3 * width), F32),
        ),
        in_specs=[SMEM] + [VMEM] * 7,
        out_specs=[VMEM] * 3,
        scratch_shapes=[
            pltpu.VMEM((rows, width), BF16),
            pltpu.VMEM((width, rows), BF16),
            pltpu.VMEM((heads * block, width), BF16),
            pltpu.VMEM((heads * block, width), BF16),
            pltpu.VMEM((rows, block), F32),
            pltpu.VMEM((rows, block), F32),
            pltpu.VMEM((rows, heads * block), BF16),
            pltpu.VMEM((rows, heads * block), BF16),
            pltpu.VMEM((rows, width), F32),
            pltpu.VMEM((rows, width), F32),
            pltpu.VMEM((rows, width), F32),
        ],
        compiler_params=pltpu.CompilerParams(vmem_limit_bytes=40 << 20),
        cost_estimate=pl.CostEstimate(
            flops=heads * rows * rows * 1280, transcendentals=heads * rows * rows // 2, bytes_accessed=8 << 20
        ),
        name="attend_back",
    )(where, own, sib, qkv, lse, *tables)


def rope_tables(rows, width):
    half = ROT // 2
    lane = jnp.arange(width, dtype=jnp.int32) % HD
    power = (lane % half).astype(F32)
    frequency = ROPE_BASE ** (-(2.0 * power) / ROT)
    angles = jnp.arange(rows, dtype=F32)[:, None] * frequency[None, :]
    cos = jnp.where(lane < ROT, jnp.cos(angles), 1.0)
    sine = jnp.sin(angles)
    plus = jnp.where((lane >= half) & (lane < ROT), sine, 0.0)
    minus = jnp.where(lane < half, -sine, 0.0)
    return (cos, plus, minus)


def local(
    tokens,
    out_grad,
    row_seq,
    seq_lengths,
    norm1_gain,
    norm1_bias,
    qkv_weight,
    qk_bias,
    v_bias,
    out_weight,
    norm2_gain,
    norm2_bias,
    gate_weight,
    up_weight,
    down_weight,
):
    line = Line()
    batches, seq_here, rows_here, depth = tokens.shape
    assert rows_here == 1
    chips = line.chips
    seq_full = seq_here * line.devices
    width = qkv_weight.shape[2]
    heads_here = width // HD
    piece = seq_here

    table = jnp.arange(seq_lengths.shape[0], dtype=jnp.int32)
    row_len = jnp.sum(jnp.where(row_seq[..., None] == table, seq_lengths, 0), axis=-1)[:, 0]
    positions = lax.axis_index("heads") * seq_here + jnp.arange(seq_here, dtype=jnp.int32)
    tables = rope_tables(seq_full, width)

    vectors = jnp.stack([norm1_gain, norm1_bias, norm2_gain, norm2_bias])
    vectors = small_gather(small_gather(vectors, "heads").reshape(4, -1), "batch")
    gain_one, shift_one, gain_two, shift_two = (vectors[i] for i in range(4))

    qkv_flat = jnp.concatenate([qkv_weight[:, j] for j in range(3)], axis=1)
    bias = jnp.concatenate([qk_bias[0].reshape(-1), qk_bias[1].reshape(-1), v_bias.reshape(-1)])
    bias = bias.astype(F32)[None, :]
    gate_full = lax.all_gather(gate_weight, "batch", axis=0, tiled=True)
    up_full = lax.all_gather(up_weight, "batch", axis=0, tiled=True)
    down_full = lax.all_gather(down_weight, "batch", axis=0, tiled=True)

    def gather_halves(block):
        own = line.gather(block)
        return (own, line.swap(own))

    def scatter_halves(product):
        received = line.swap(product(1).astype(BF16))
        summed = (product(0) + received.astype(F32)).astype(BF16)
        return line.scatter([summed[k * piece : (k + 1) * piece] for k in range(chips)])

    class Row:
        pass

    rows = []
    for r in range(batches):
        row = Row()
        row.length = row_len[r]
        row.where = jnp.stack([line.chip, line.core, row.length]).astype(jnp.int32)
        row.valid = (positions < row.length).astype(F32)[:, None]
        row.grad_y = (out_grad[r, :, 0].astype(F32) * row.valid).astype(BF16)
        row.inputs = tokens[r, :, 0].astype(F32)
        normed, row.unit_one, row.inverse_one = row_norm(row.inputs, gain_one, shift_one)
        row.normed_one = normed.astype(BF16)
        rows.append(row)

    def stage_attend(row, *earlier):
        raw = [dot(after(x, *earlier), qkv_flat, 1, 0) for x in row.ones]
        *row.attn, row.qkv, row.lse = attend(row.where, *raw, bias, tables, chips, heads_here)
        row.branch = scatter_halves(lambda s: dot(row.attn[s], out_weight, 1, 0))
        return row.attn[0]

    def stage_norm(row, *earlier):
        row.state = row.inputs + after(row.branch, *earlier)
        normed, row.unit_two, row.inverse_two = row_norm(row.state, gain_two, shift_two)
        row.normed_two = normed.astype(BF16)
        row.twos = gather_halves(row.normed_two)
        return row.normed_two

    def stage_mlp(row, *earlier):
        row.inner, row.grad_gate, row.grad_up = [], [], []
        for s in range(2):
            twos = after(row.twos[s], *earlier)
            gate = dot(twos, gate_full, 1, 0)
            up = dot(twos, up_full, 1, 0)
            sigma = jax.nn.sigmoid(gate)
            silu = gate * sigma
            row.inner.append((silu * up).astype(BF16))
            grad_inner = dot(row.grads[s], down_full, 1, 0)
            row.grad_gate.append((grad_inner * up * sigma * (1.0 + gate * (1.0 - sigma))).astype(BF16))
            row.grad_up.append((grad_inner * silu).astype(BF16))
        row.grad_two = scatter_halves(
            lambda s: dot(row.grad_gate[s], gate_full, 1, 1) + dot(row.grad_up[s], up_full, 1, 1)
        )
        return row.grad_gate[0]

    def stage_state(row, *earlier):
        row.grad_two = after(row.grad_two, *earlier)
        row.grad_state = row.grad_y.astype(F32) + norm_back(
            row.grad_two, row.unit_two, row.inverse_two, gain_two
        )
        low = row.grad_state.astype(BF16)
        row.states = gather_halves(low)
        return low

    def stage_back(row, *earlier):
        grad_attn = [dot(after(x, *earlier), out_weight, 1, 1).astype(BF16) for x in row.states]
        *row.grad_qkv, bias_grad = attend_back(
            row.where, *grad_attn, row.qkv, row.lse, tables, chips, heads_here
        )
        row.bias_grad = bias_grad[0]
        row.grad_one = scatter_halves(lambda s: dot(row.grad_qkv[s], qkv_flat, 1, 1))
        return row.grad_qkv[0]

    def stage_down(row, *earlier):
        row.inner = [after(x, *earlier) for x in row.inner]
        row.mlp = scatter_halves(lambda s: dot(row.inner[s], down_full, 1, 1))

    def stage_end(row):
        row.input_grad = row.grad_state + norm_back(
            row.grad_one, row.unit_one, row.inverse_one, gain_one
        )
        row.norms = jnp.stack(
            [
                jnp.sum(row.grad_one * row.unit_one, axis=0),
                jnp.sum(row.grad_one, axis=0),
                jnp.sum(row.grad_two * row.unit_two, axis=0),
                jnp.sum(row.grad_two, axis=0),
            ]
        )
        row.output = ((row.state + row.mlp) * row.valid).astype(BF16)

    first, second = rows
    for row in rows:
        row.ones = gather_halves(row.normed_one)
        row.grads = gather_halves(row.grad_y)
    token = stage_attend(first)
    token = stage_attend(second, token)
    token = stage_norm(first, token)
    token = stage_norm(second, token)
    token = stage_mlp(first, token)
    token = stage_mlp(second, token)
    stage_down(first, token)
    stage_down(second, token)
    token = stage_state(first, token)
    token = stage_state(second, token)
    token = stage_back(first, token)
    token = stage_back(second, token)
    for row in rows:
        stage_end(row)

    def weight_grad(left, right, dim):
        total = None
        for row in rows:
            for s in range(2):
                term = dot(getattr(row, left)[s], getattr(row, right)[s], 0, 0)
                total = term if total is None else total + term
        low = total.astype(BF16)
        return lax.psum_scatter(low, "batch", scatter_dimension=dim, tiled=True).astype(F32)

    down_grad = weight_grad("grads", "inner", 0)
    gate_grad = weight_grad("twos", "grad_gate", 0)
    up_grad = weight_grad("twos", "grad_up", 0)
    out_grad_w = weight_grad("attn", "states", 1)
    qkv_grad = weight_grad("ones", "grad_qkv", 0)
    qkv_grad = jnp.stack([qkv_grad[:, j * width : (j + 1) * width] for j in range(3)], axis=1)

    bias_sum = functools.reduce(jnp.add, [row.bias_grad for row in rows])
    bias_sum = small_scatter(bias_sum.reshape(3 * heads_here, HD), "batch", 1)
    bias_sum = bias_sum.reshape(3, heads_here, -1)
    norm_sum = functools.reduce(jnp.add, [row.norms for row in rows])
    norm_sum = small_scatter(small_scatter(norm_sum, "batch", 1), "heads", 1)
    return (
        jnp.stack([row.output for row in rows])[:, :, None],
        jnp.stack([row.input_grad.astype(BF16) for row in rows])[:, :, None],
        norm_sum[0],
        norm_sum[1],
        qkv_grad,
        bias_sum[:2],
        bias_sum[2],
        out_grad_w,
        norm_sum[2],
        norm_sum[3],
        gate_grad,
        up_grad,
        down_grad,
    )


def solution(mesh):
    placed = (
        P(None, "heads", "batch", None),
        P(None, "heads", "batch", None),
        P(None, "batch"),
        P(),
        P(("batch", "heads")),
        P(("batch", "heads")),
        P(None, None, "heads"),
        P(None, "heads", None),
        P("heads", None),
        P("heads", None),
        P(("batch", "heads")),
        P(("batch", "heads")),
        P("batch", "heads"),
        P("batch", "heads"),
        P("batch", "heads"),
    )
    return jax.shard_map(
        local,
        mesh=mesh,
        in_specs=placed,
        out_specs=(
            P(None, "heads", "batch", None),
            P(None, "heads", "batch", None),
            P(("batch", "heads")),
            P(("batch", "heads")),
            P("batch", None, "heads"),
            P(None, "heads", "batch"),
            P("heads", "batch"),
            P("heads", "batch"),
            P(("batch", "heads")),
            P(("batch", "heads")),
            P("batch", "heads"),
            P("batch", "heads"),
            P("batch", "heads"),
        ),
        check_vma=False,
    )
```

time: 1300 us -> 878 us (0.68)
  waiting for transfers between devices: 740 us -> 247 us
  starting transfers between devices: 13.5 us -> 289 us
  blocking collectives: 89.6 us -> 0 us
  local copies, waits for them, and re-layouts: 91.6 us -> 14.4 us
  matrix products: 234 us -> 197 us
  Pallas kernels: 0 us -> 35.5 us
  other arithmetic: 92.2 us -> 65 us
    reduce_scatter x13 -> x5, waiting for transfers between devices: 410 us -> 0.01 us  [weight_grad(): lax.psum_scatter(low, 'batch', scatter_dimension=dim, tiled=True)]
    all_gather x11 -> x3, waiting for transfers between devices: 326 us -> 0.01 us  [the longest x1 0.01 us: local(): up_full = lax.all_gather(up_weight, 'batch', axis=0, tiled=True)]
    ppermute x0 -> x135, starting transfers between devices: none -> 289 us  [the longest x96 242 us: hop(): return lax.ppermute(value, 'heads', pairs)]
    ppermute x0 -> x135, waiting for transfers between devices: none -> 245 us  [the longest x96 233 us: hop(): return lax.ppermute(value, 'heads', pairs)]
    unnamed x3 -> x0, blocking collectives: 89.6 us -> none
    dot_general x65 -> x60, matrix products: 234 us -> 197 us  [dot(): lax.dot_general(a, b, (((ca,), (cb,)), ((), ())), preferred_element_type=...]
    pallas_call x0 -> x4, Pallas kernels: none -> 35.5 us  [the longest x2 20.7 us: attend_back(): pl.pallas_call(functools.partial(backward_kernel, chips, heads), out_shap...]
    another operation x32 -> x1, local copies, waits for them, and re-layouts: 28.1 us -> 0.16 us  [local(): jnp.stack([qkv_grad[:, j * width:(j + 1) * width] for j in range(3)], axi...]
  transfers between devices with their start and end apart: 24 -> 143, of which waited for: 19 -> 51; matrix products, arithmetic and copies ran while one was open for 22% -> 29% of each run, Pallas kernels for 0% -> 3%
where the time goes in v1:
time: 878 us; the launch traced here: 866 us
  starting transfers between devices  289 us (33%)
  waiting for transfers between devices  247 us (28%)
  matrix products  197 us (22%)
  other arithmetic  65 us (7%)
  Pallas kernels  35.5 us (4%)
  between operations  18.4 us (2%)
  local copies, waits for them, and re-layouts  14.4 us (2%)
    ppermute x96, starting transfers between devices, hop(): return lax.ppermute(value, 'heads', pairs)  242 us
    ppermute x96, waiting for transfers between devices, hop(): return lax.ppermute(value, 'heads', pairs)  233 us
    dot_general x60, matrix products, dot(): lax.dot_general(a, b, (((ca,), (cb,)), ((), ())), preferred_element_type=...  197 us
    ppermute x23, starting transfers between devices, shifts(): lax.ppermute(value_of(k), axis, [(i, (i + k) % n) for i in range(n)])  43.4 us
    pallas_call x2, Pallas kernels, attend_back(): pl.pallas_call(functools.partial(backward_kernel, chips, heads), out_shap...  20.7 us
  transfers between devices with their start and end apart: 143, of which 51 were waited for; matrix products, arithmetic and copies ran while one was open for 29% of the time, Pallas kernels for 3%

profile of v1, /device:TPU:0, one launch (start us, length us, event | category | flops | bytes accessed | tf_op | source)
XLA Modules:
  0.0 866.3 jit_solution(8549805643147574826)
XLA Ops:
  72.7 8.4 collective-permute-done.12
  84.9 7.5 collective-permute-done.26
  95.5 8.0 collective-permute-done.13
  110.1 13.1 %collective-permute-done.27 = bf16[128,2048]{1,0:T(8,128)(2,1)S(1)} collective-permute-done((bf16[128,2048]{1,0:T(8,128)(2,1)}, bf16[128,2048]{1,0:T(8,128)(2,1)S(1)}, u32[]{:S(2)}, u32[]{:S(2)}) %collective-permute-start.27) | collective-permute-done | bytes 524320 | tf_op jit(solution)/shard_map/ppermute | solution.py:53
  133.2 11.5 %collective-permute-done.45 = bf16[128,2048]{1,0:T(8,128)(2,1)S(1)} collective-permute-done((bf16[128,2048]{1,0:T(8,128)(2,1)S(1)}, bf16[128,2048]{1,0:T(8,128)(2,1)S(1)}, u32[]{:S(2)}, u32[]{:S(2)}) %collective-permute-start.45) | collective-permute-done | bytes 524320 | tf_op jit(solution)/shard_map/ppermute | solution.py:53
  159.7 9.1 %attend.3 = (bf16[512,256]{1,0:T(8,128)(2,1)S(1)}, bf16[512,256]{1,0:T(8,128)(2,1)S(1)}, bf16[1024,768]{1,0:T(8,128)(2,1)S(1)}, f32[8,1024]{1,0:T(8,128)S(1)}) custom-call(s32[3]{0:T(128)S(1)} %get-tuple-element.235.where_ref, f32[512,768]{1,0:T(8,128)S(1)} %fusion.94.own_ref, f32[512,768]{1,0:T(8,128)S(1)} %fusion.93.sib_ref, ...), custom_call_target="tpu_custom_call" | custom-call | flops 2147483648 | bytes 8388608 | tf_op jit(solution)/shard_map/attend/pallas_call | solution.py:274
  180.9 9.4 %collective-permute-done.18 = bf16[128,2048]{1,0:T(8,128)(2,1)S(1)} collective-permute-done((bf16[128,2048]{1,0:T(8,128)(2,1)S(1)}, bf16[128,2048]{1,0:T(8,128)(2,1)S(1)}, u32[]{:S(2)}, u32[]{:S(2)}) %collective-permute-start.18) | collective-permute-done | bytes 524320 | tf_op jit(solution)/shard_map/ppermute | solution.py:53
  225.7 10.6 %collective-permute-start.40 = (bf16[128,2048]{1,0:T(8,128)(2,1)S(1)}, bf16[128,2048]{1,0:T(8,128)(2,1)S(1)}, u32[]{:S(2)}, u32[]{:S(2)}) collective-permute-start(bf16[128,2048]{1,0:T(8,128)(2,1)S(1)} %get-tuple-element.188), channel_id=1, source_target_pairs={{0,2},{1,3},{2,4},{3,5},{4,6},{5,7},{8,10},{9,11},{10,12},{11,13},... | collective-permute-start | bytes 1572872 | tf_op jit(solution)/shard_map/ppermute | solution.py:53
  237.2 8.9 %collective-permute-start.31 = (bf16[128,2048]{1,0:T(8,128)(2,1)S(1)}, bf16[128,2048]{1,0:T(8,128)(2,1)S(1)}, u32[]{:S(2)}, u32[]{:S(2)}) collective-permute-start(bf16[128,2048]{1,0:T(8,128)(2,1)S(1)} %add_convert_fusion.29), channel_id=1, source_target_pairs={{0,2},{1,3},{2,4},{3,5},{4,6},{5,7},{8,10},{9,11},{10,12},{11,13},... | collective-permute-start | bytes 1572872 | tf_op jit(solution)/shard_map/ppermute | solution.py:53
  250.2 7.9 collective-permute-start.50
  273.6 7.3 collective-permute-done.33
  282.9 9.2 %collective-permute-done.52 = bf16[128,2048]{1,0:T(8,128)(2,1)S(1)} collective-permute-done((bf16[128,2048]{1,0:T(8,128)(2,1)S(1)}, bf16[128,2048]{1,0:T(8,128)(2,1)S(1)}, u32[]{:S(2)}, u32[]{:S(2)}) %collective-permute-start.52) | collective-permute-done | bytes 524320 | tf_op jit(solution)/shard_map/ppermute | solution.py:53
  294.5 9.5 %collective-permute-done.34 = bf16[128,2048]{1,0:T(8,128)(2,1)S(1)} collective-permute-done((bf16[128,2048]{1,0:T(8,128)(2,1)S(1)}, bf16[128,2048]{1,0:T(8,128)(2,1)S(1)}, u32[]{:S(2)}, u32[]{:S(2)}) %collective-permute-start.34) | collective-permute-done | bytes 524320 | tf_op jit(solution)/shard_map/ppermute | solution.py:53
  305.7 8.4 collective-permute-done.53
  326.2 6.8 multiply_convert_fusion.5
  436.7 6.1 add_convert_fusion.6
  479.8 10.0 %collective-permute-start.81 = (bf16[128,2048]{1,0:T(8,128)(2,1)S(1)}, bf16[128,2048]{1,0:T(8,128)(2,1)S(1)}, u32[]{:S(2)}, u32[]{:S(2)}) collective-permute-start(bf16[128,2048]{1,0:T(8,128)(2,1)S(1)} %get-tuple-element.160), channel_id=1, source_target_pairs={{0,2},{1,3},{2,4},{3,5},{8,10},{9,11},{10,12},{11,13},{16,18},{17,... | collective-permute-start | bytes 1572872 | tf_op jit(solution)/shard_map/ppermute | solution.py:53
  490.3 6.7 collective-permute-start.84
  513.5 9.3 %collective-permute-start.99 = (bf16[128,2048]{1,0:T(8,128)(2,1)S(1)}, bf16[128,2048]{1,0:T(8,128)(2,1)S(1)}, u32[]{:S(2)}, u32[]{:S(2)}) collective-permute-start(bf16[128,2048]{1,0:T(8,128)(2,1)S(1)} %get-tuple-element.165), channel_id=1, source_target_pairs={{2,0},{3,1},{4,2},{5,3},{6,4},{7,5},{10,8},{11,9},{12,10},{13,11},... | collective-permute-start | bytes 1572872 | tf_op jit(solution)/shard_map/ppermute | solution.py:53
  541.5 7.8 collective-permute-done.85
  549.3 11.2 %collective-permute-start.66 = (bf16[128,2048]{1,0:T(8,128)(2,1)S(1)}, bf16[128,2048]{1,0:T(8,128)(2,1)S(1)}, u32[]{:S(2)}, u32[]{:S(2)}) collective-permute-start(bf16[128,2048]{1,0:T(8,128)(2,1)S(1)} %get-tuple-element.170), channel_id=1, source_target_pairs={{0,2},{1,3},{2,4},{3,5},{4,6},{5,7},{8,10},{9,11},{10,12},{11,13},... | collective-permute-start | bytes 1572872 | tf_op jit(solution)/shard_map/ppermute | solution.py:53
  562.6 7.4 collective-permute-start.74
  583.9 6.8 collective-permute-start.108
  603.8 7.8 collective-permute-done.86
  613.5 7.8 collective-permute-done.87
  624.0 12.0 %collective-permute-done.110 = bf16[128,2048]{1,0:T(8,128)(2,1)S(1)} collective-permute-done((bf16[128,2048]{1,0:T(8,128)(2,1)S(1)}, bf16[128,2048]{1,0:T(8,128)(2,1)S(1)}, u32[]{:S(2)}, u32[]{:S(2)}) %collective-permute-start.110) | collective-permute-done | bytes 524320 | tf_op jit(solution)/shard_map/ppermute | solution.py:53
  637.3 9.9 %collective-permute-done.88 = bf16[128,2048]{1,0:T(8,128)(2,1)S(1)} collective-permute-done((bf16[128,2048]{1,0:T(8,128)(2,1)S(1)}, bf16[128,2048]{1,0:T(8,128)(2,1)S(1)}, u32[]{:S(2)}, u32[]{:S(2)}) %collective-permute-start.88) | collective-permute-done | bytes 524320 | tf_op jit(solution)/shard_map/ppermute | solution.py:53
  648.8 15.9 %collective-permute-done.89 = bf16[128,2048]{1,0:T(8,128)(2,1)S(1)} collective-permute-done((bf16[128,2048]{1,0:T(8,128)(2,1)S(1)}, bf16[128,2048]{1,0:T(8,128)(2,1)S(1)}, u32[]{:S(2)}, u32[]{:S(2)}) %collective-permute-start.89) | collective-permute-done | bytes 524320 | tf_op jit(solution)/shard_map/ppermute | solution.py:53
  684.7 7.0 attend_back.2
  696.9 13.7 %attend_back.3 = (bf16[512,768]{1,0:T(8,128)(2,1)S(1)}, bf16[512,768]{1,0:T(8,128)(2,1)S(1)}, f32[8,768]{1,0:T(8,128)S(1)}) custom-call(s32[3]{0:T(128)S(1)} %copy-done.16, bf16[512,256]{1,0:T(8,128)(2,1)S(1)} %convolution_convert_fusion.7.own_ref, bf16[512,256]{1,0:T(8,128)(2,1)S(1)} %convolution_convert_fusion.6.sib_ref, bf16[1024,768]{1,0:T(8,128)(2,1)S(1)} %copy-done.20, ...), custom_call_target="tpu_custom_call" | custom-call | flops 5368709120 | bytes 8388608 | tf_op jit(solution)/shard_map/attend_back/pallas_call | solution.py:301
  724.7 6.1 fusion.127
  829.2 7.9 collective-permute-start.123
  (774 shorter events, 559.1 us)
Async XLA Ops:
  7.2 308.5 %all-gather.4.cloned.1.call-start = ((), (), s32[]{:S(2)}) async-start(), calls=%async_computation.5 | async-start | bytes 3604480 | tf_op jit(solution)/shard_map/all_gather | solution.py:382
  8.0 313.0 %all-gather.6.cloned.1.call-start = ((), (), s32[]{:S(2)}) async-start(), calls=%async_computation.6 | async-start | bytes 3604480 | tf_op jit(solution)/shard_map/all_gather | solution.py:383
  8.7 317.4 %all-gather.8.cloned.1.call-start = ((), (), s32[]{:S(2)}) async-start(), calls=%async_computation.7 | async-start | bytes 3604480 | tf_op jit(solution)/shard_map/all_gather | solution.py:384
  17.4 657.4 %reduce-scatter.10.cloned.1.call-start = ((), (), s32[]{:S(2)}) async-start(), calls=%async_computation.10 | async-start | bytes 3604480 | tf_op jit(solution)/shard_map/reduce_scatter | solution.py:502
  24.1 104.0 %collective-permute-start.56 = (bf16[128,2048]{1,0:T(8,128)(2,1)}, bf16[128,2048]{1,0:T(8,128)(2,1)}, u32[]{:S(2)}, u32[]{:S(2)}) collective-permute-start(bf16[128,2048]{1,0:T(8,128)(2,1)} %get-tuple-element.203), channel_id=1, source_target_pairs={{0,2},{1,3},{2,4},{3,5},{4,6},{5,7},{8,10},{9,11},{10,12},{11,13},... | collective-permute-start | bytes 1572872 | tf_op jit(solution)/shard_map/ppermute | solution.py:53
  83.6 45.8 %collective-permute-start.57 = (bf16[128,2048]{1,0:T(8,128)(2,1)}, bf16[128,2048]{1,0:T(8,128)(2,1)S(1)}, u32[]{:S(2)}, u32[]{:S(2)}) collective-permute-start(bf16[128,2048]{1,0:T(8,128)(2,1)} %get-tuple-element.203), channel_id=1, source_target_pairs={{2,0},{3,1},{4,2},{5,3},{6,4},{7,5},{10,8},{11,9},{12,10},{13,11},... | collective-permute-start | bytes 1572872 | tf_op jit(solution)/shard_map/ppermute | solution.py:53
  93.1 30.1 %collective-permute-start.27 = (bf16[128,2048]{1,0:T(8,128)(2,1)}, bf16[128,2048]{1,0:T(8,128)(2,1)S(1)}, u32[]{:S(2)}, u32[]{:S(2)}) collective-permute-start(bf16[128,2048]{1,0:T(8,128)(2,1)} %collective-permute-done.26), channel_id=1, source_target_pairs={{2,0},{3,1},{10,8},{11,9},{18,16},{19,17},{26,24},{27,25}} | collective-permute-start | bytes 1572872 | tf_op jit(solution)/shard_map/ppermute | solution.py:53
  105.1 41.8 %collective-permute-start.16 = (bf16[512,2048]{1,0:T(8,128)(2,1)S(1)}, bf16[512,2048]{1,0:T(8,128)(2,1)S(1)}, u32[]{:S(2)}, u32[]{:S(2)}) collective-permute-start(bf16[512,2048]{1,0:T(8,128)(2,1)S(1)} %pad_maximum_fusion.1), channel_id=1, source_target_pairs={{0,1},{1,0},{2,3},{3,2},{4,5},{5,4},{6,7},{7,6},{8,9},{9,8},{10,11... | collective-permute-start | bytes 6291464 | tf_op jit(solution)/shard_map/ppermute | solution.py:57
  124.1 32.9 %collective-permute-start.30 = (bf16[512,2048]{1,0:T(8,128)(2,1)S(1)}, bf16[512,2048]{1,0:T(8,128)(2,1)S(1)}, u32[]{:S(2)}, u32[]{:S(2)}) collective-permute-start(bf16[512,2048]{1,0:T(8,128)(2,1)S(1)} %pad_maximum_fusion.2), channel_id=1, source_target_pairs={{0,1},{1,0},{2,3},{3,2},{4,5},{5,4},{6,7},{7,6},{8,9},{9,8},{10,11... | collective-permute-start | bytes 6291464 | tf_op jit(solution)/shard_map/ppermute | solution.py:57
  131.9 37.7 %collective-permute-start.58 = (bf16[128,2048]{1,0:T(8,128)(2,1)S(1)}, bf16[128,2048]{1,0:T(8,128)(2,1)S(1)}, u32[]{:S(2)}, u32[]{:S(2)}) collective-permute-start(bf16[128,2048]{1,0:T(8,128)(2,1)S(1)} %collective-permute-done.57), channel_id=1, source_target_pairs={{2,0},{3,1},{4,2},{5,3},{10,8},{11,9},{12,10},{13,11},{18,16},{19,... | collective-permute-start | bytes 1572872 | tf_op jit(solution)/shard_map/ppermute | solution.py:53
  170.2 90.8 %collective-permute-start.59 = (bf16[128,2048]{1,0:T(8,128)(2,1)S(1)}, bf16[128,2048]{1,0:T(8,128)(2,1)S(1)}, u32[]{:S(2)}, u32[]{:S(2)}) collective-permute-start(bf16[128,2048]{1,0:T(8,128)(2,1)S(1)} %collective-permute-done.58), channel_id=1, source_target_pairs={{2,0},{3,1},{10,8},{11,9},{18,16},{19,17},{26,24},{27,25}} | collective-permute-start | bytes 1572872 | tf_op jit(solution)/shard_map/ppermute | solution.py:53
  261.0 93.3 %collective-permute-start.92 = (bf16[512,2048]{1,0:T(8,128)(2,1)}, bf16[512,2048]{1,0:T(8,128)(2,1)}, u32[]{:S(2)}, u32[]{:S(2)}) collective-permute-start(bf16[512,2048]{1,0:T(8,128)(2,1)} %pad_maximum_fusion.4), channel_id=1, source_target_pairs={{0,1},{1,0},{2,3},{3,2},{4,5},{5,4},{6,7},{7,6},{8,9},{9,8},{10,11... | collective-permute-start | bytes 6291464 | tf_op jit(solution)/shard_map/ppermute | solution.py:57
  273.6 95.8 %collective-permute-start.78 = (bf16[512,2048]{1,0:T(8,128)(2,1)}, bf16[512,2048]{1,0:T(8,128)(2,1)}, u32[]{:S(2)}, u32[]{:S(2)}) collective-permute-start(bf16[512,2048]{1,0:T(8,128)(2,1)} %pad_maximum_fusion.6), channel_id=1, source_target_pairs={{0,1},{1,0},{2,3},{3,2},{4,5},{5,4},{6,7},{7,6},{8,9},{9,8},{10,11... | collective-permute-start | bytes 6291464 | tf_op jit(solution)/shard_map/ppermute | solution.py:57
  305.6 41.8 %collective-permute-start.62 = (bf16[512,2048]{1,0:T(8,128)(2,1)}, bf16[512,2048]{1,0:T(8,128)(2,1)}, u32[]{:S(2)}, u32[]{:S(2)}) collective-permute-start(bf16[512,2048]{1,0:T(8,128)(2,1)} %pad_maximum_fusion.3), channel_id=1, source_target_pairs={{0,1},{1,0},{2,3},{3,2},{4,5},{5,4},{6,7},{7,6},{8,9},{9,8},{10,11... | collective-permute-start | bytes 6291464 | tf_op jit(solution)/shard_map/ppermute | solution.py:57
  315.7 31.7 %collective-permute-start.70 = (bf16[512,2048]{1,0:T(8,128)(2,1)}, bf16[512,2048]{1,0:T(8,128)(2,1)}, u32[]{:S(2)}, u32[]{:S(2)}) collective-permute-start(bf16[512,2048]{1,0:T(8,128)(2,1)} %pad_maximum_fusion.5), channel_id=1, source_target_pairs={{0,1},{1,0},{2,3},{3,2},{4,5},{5,4},{6,7},{7,6},{8,9},{9,8},{10,11... | collective-permute-start | bytes 6291464 | tf_op jit(solution)/shard_map/ppermute | solution.py:57
  381.2 296.0 %reduce-scatter.12.cloned.1.call-start = ((), (), s32[]{:S(2)}) async-start(), calls=%async_computation.11 | async-start | bytes 3604480 | tf_op jit(solution)/shard_map/reduce_scatter | solution.py:502
  398.7 280.9 %reduce-scatter.14.cloned.1.call-start = ((), (), s32[]{:S(2)}) async-start(), calls=%async_computation.12 | async-start | bytes 3604480 | tf_op jit(solution)/shard_map/reduce_scatter | solution.py:502
  421.4 29.4 %collective-permute-start.63 = (bf16[512,2048]{1,0:T(8,128)(2,1)}, bf16[512,2048]{1,0:T(8,128)(2,1)}, u32[]{:S(2)}, u32[]{:S(2)}) collective-permute-start(bf16[512,2048]{1,0:T(8,128)(2,1)} %convolution_convert_fusion.5), channel_id=1, source_target_pairs={{0,1},{1,0},{2,3},{3,2},{4,5},{5,4},{6,7},{7,6},{8,9},{9,8},{10,11... | collective-permute-start | bytes 6291464 | tf_op jit(solution)/shard_map/ppermute | solution.py:57
  425.5 33.7 %collective-permute-start.71 = (bf16[512,2048]{1,0:T(8,128)(2,1)}, bf16[512,2048]{1,0:T(8,128)(2,1)}, u32[]{:S(2)}, u32[]{:S(2)}) collective-permute-start(bf16[512,2048]{1,0:T(8,128)(2,1)} %convolution_convert_fusion.4), channel_id=1, source_target_pairs={{0,1},{1,0},{2,3},{3,2},{4,5},{5,4},{6,7},{7,6},{8,9},{9,8},{10,11... | collective-permute-start | bytes 6291464 | tf_op jit(solution)/shard_map/ppermute | solution.py:57
  435.6 367.1 %reduce-scatter.8.cloned.1.call-start = ((), (), s32[]{:S(2)}) async-start(), calls=%async_computation.9 | async-start | bytes 1310720 | tf_op jit(solution)/shard_map/reduce_scatter | solution.py:502
  469.8 31.8 %collective-permute-start.95 = (bf16[128,2048]{1,0:T(8,128)(2,1)S(1)}, bf16[128,2048]{1,0:T(8,128)(2,1)S(1)}, u32[]{:S(2)}, u32[]{:S(2)}) collective-permute-start(bf16[128,2048]{1,0:T(8,128)(2,1)S(1)} %get-tuple-element.166), channel_id=1, source_target_pairs={{0,2},{1,3},{2,4},{3,5},{8,10},{9,11},{10,12},{11,13},{16,18},{17,... | collective-permute-start | bytes 1572872 | tf_op jit(solution)/shard_map/ppermute | solution.py:53
  479.8 33.0 %collective-permute-start.81 = (bf16[128,2048]{1,0:T(8,128)(2,1)S(1)}, bf16[128,2048]{1,0:T(8,128)(2,1)S(1)}, u32[]{:S(2)}, u32[]{:S(2)}) collective-permute-start(bf16[128,2048]{1,0:T(8,128)(2,1)S(1)} %get-tuple-element.160), channel_id=1, source_target_pairs={{0,2},{1,3},{2,4},{3,5},{8,10},{9,11},{10,12},{11,13},{16,18},{17,... | collective-permute-start | bytes 1572872 | tf_op jit(solution)/shard_map/ppermute | solution.py:53
  502.3 33.0 %collective-permute-start.73 = (bf16[128,2048]{1,0:T(8,128)(2,1)S(1)}, bf16[128,2048]{1,0:T(8,128)(2,1)S(1)}, u32[]{:S(2)}, u32[]{:S(2)}) collective-permute-start(bf16[128,2048]{1,0:T(8,128)(2,1)S(1)} %get-tuple-element.178), channel_id=1, source_target_pairs={{0,2},{1,3},{2,4},{3,5},{8,10},{9,11},{10,12},{11,13},{16,18},{17,... | collective-permute-start | bytes 1572872 | tf_op jit(solution)/shard_map/ppermute | solution.py:53
  513.5 49.1 %collective-permute-start.99 = (bf16[128,2048]{1,0:T(8,128)(2,1)S(1)}, bf16[128,2048]{1,0:T(8,128)(2,1)S(1)}, u32[]{:S(2)}, u32[]{:S(2)}) collective-permute-start(bf16[128,2048]{1,0:T(8,128)(2,1)S(1)} %get-tuple-element.165), channel_id=1, source_target_pairs={{2,0},{3,1},{4,2},{5,3},{6,4},{7,5},{10,8},{11,9},{12,10},{13,11},... | collective-permute-start | bytes 1572872 | tf_op jit(solution)/shard_map/ppermute | solution.py:53
  525.3 35.2 %collective-permute-start.82 = (bf16[128,2048]{1,0:T(8,128)(2,1)S(1)}, bf16[128,2048]{1,0:T(8,128)(2,1)S(1)}, u32[]{:S(2)}, u32[]{:S(2)}) collective-permute-start(bf16[128,2048]{1,0:T(8,128)(2,1)S(1)} %get-tuple-element.158), channel_id=1, source_target_pairs={{0,2},{1,3},{2,4},{3,5},{4,6},{5,7},{8,10},{9,11},{10,12},{11,13},... | collective-permute-start | bytes 1572872 | tf_op jit(solution)/shard_map/ppermute | solution.py:53
  535.3 34.8 %collective-permute-start.96 = (bf16[128,2048]{1,0:T(8,128)(2,1)S(1)}, bf16[128,2048]{1,0:T(8,128)(2,1)S(1)}, u32[]{:S(2)}, u32[]{:S(2)}) collective-permute-start(bf16[128,2048]{1,0:T(8,128)(2,1)S(1)} %get-tuple-element.164), channel_id=1, source_target_pairs={{0,2},{1,3},{2,4},{3,5},{4,6},{5,7},{8,10},{9,11},{10,12},{11,13},... | collective-permute-start | bytes 1572872 | tf_op jit(solution)/shard_map/ppermute | solution.py:53
  539.7 30.6 %collective-permute-start.69 = (bf16[128,2048]{1,0:T(8,128)(2,1)S(1)}, bf16[128,2048]{1,0:T(8,128)(2,1)S(1)}, u32[]{:S(2)}, u32[]{:S(2)}) collective-permute-start(bf16[128,2048]{1,0:T(8,128)(2,1)S(1)} %get-tuple-element.171), channel_id=1, source_target_pairs={{2,0},{3,1},{4,2},{5,3},{6,4},{7,5},{10,8},{11,9},{12,10},{13,11},... | collective-permute-start | bytes 1572872 | tf_op jit(solution)/shard_map/ppermute | solution.py:53
  622.6 43.1 %collective-permute-start.113 = (bf16[128,2048]{1,0:T(8,128)(2,1)S(1)}, bf16[128,2048]{1,0:T(8,128)(2,1)S(1)}, u32[]{:S(2)}, u32[]{:S(2)}) collective-permute-start(bf16[128,2048]{1,0:T(8,128)(2,1)S(1)} %collective-permute-done.112), channel_id=1, source_target_pairs={{4,6},{5,7},{12,14},{13,15},{20,22},{21,23},{28,30},{29,31}} | collective-permute-start | bytes 1572872 | tf_op jit(solution)/shard_map/ppermute | solution.py:53
  636.0 29.7 %collective-permute-start.111 = (bf16[128,2048]{1,0:T(8,128)(2,1)S(1)}, bf16[128,2048]{1,0:T(8,128)(2,1)S(1)}, u32[]{:S(2)}, u32[]{:S(2)}) collective-permute-start(bf16[128,2048]{1,0:T(8,128)(2,1)S(1)} %collective-permute-done.110), channel_id=1, source_target_pairs={{2,0},{3,1},{10,8},{11,9},{18,16},{19,17},{26,24},{27,25}} | collective-permute-start | bytes 1572872 | tf_op jit(solution)/shard_map/ppermute | solution.py:53
  713.7 39.7 %collective-permute-start.115 = (bf16[512,2048]{1,0:T(8,128)(2,1)}, bf16[512,2048]{1,0:T(8,128)(2,1)}, u32[]{:S(2)}, u32[]{:S(2)}) collective-permute-start(bf16[512,2048]{1,0:T(8,128)(2,1)} %convolution_convert_fusion.2), channel_id=1, source_target_pairs={{0,1},{1,0},{2,3},{3,2},{4,5},{5,4},{6,7},{7,6},{8,9},{9,8},{10,11... | collective-permute-start | bytes 6291464 | tf_op jit(solution)/shard_map/ppermute | solution.py:57
  716.9 29.5 %collective-permute-start.101 = (bf16[512,2048]{1,0:T(8,128)(2,1)}, bf16[512,2048]{1,0:T(8,128)(2,1)}, u32[]{:S(2)}, u32[]{:S(2)}) collective-permute-start(bf16[512,2048]{1,0:T(8,128)(2,1)} %convolution_convert_fusion.3), channel_id=1, source_target_pairs={{0,1},{1,0},{2,3},{3,2},{4,5},{5,4},{6,7},{7,6},{8,9},{9,8},{10,11... | collective-permute-start | bytes 6291464 | tf_op jit(solution)/shard_map/ppermute | solution.py:57
  724.5 131.8 %reduce-scatter.6.cloned.1.call-start = ((), (), s32[]{:S(2)}) async-start(), calls=%async_computation.8 | async-start | bytes 3932160 | tf_op jit(solution)/shard_map/reduce_scatter | solution.py:502
  (265 other events, 4569.5 us)
Sparse Core Ops, SparseCore 0:
  9.9 44.7 all-gather.3
  56.5 41.6 all-gather.5
  100.0 41.6 all-gather.7
  381.3 41.8 reduce-scatter.9
  426.2 41.7 reduce-scatter.11
  470.8 41.7 reduce-scatter.13
  724.6 32.2 reduce-scatter.7
  760.2 44.2 reduce-scatter.5

commit v2 on v1

--- a/solution.py
+++ b/solution.py
@@ -55,6 +55,27 @@
     def swap(self, value):
         pairs = [(2 * i + c, 2 * i + 1 - c) for i in range(self.chips) for c in range(2)]
         return lax.ppermute(value, "heads", pairs)
+
+    def place(self, k, core):
+        return 2 * ((self.chip - k) % self.chips) + core
+
+    def pick(self, full):
+        size = full.shape[0] // self.devices
+        return tuple(
+            jnp.concatenate(
+                [lax.dynamic_slice_in_dim(full, self.place(k, core) * size, size, 0) for k in range(self.chips)]
+            )
+            for core in (self.core, 1 - self.core)
+        )
+
+    def spread(self, halves):
+        size = halves[0].shape[0] // self.chips
+        full = jnp.zeros((size * self.devices, halves[0].shape[1]), halves[0].dtype)
+        for half, core in zip(halves, (self.core, 1 - self.core)):
+            for k in range(self.chips):
+                rows = half[k * size : (k + 1) * size]
+                full = lax.dynamic_update_slice_in_dim(full, rows, self.place(k, core) * size, 0)
+        return full
 
     def gather(self, block):
         n = self.chips
@@ -456,8 +477,9 @@
         return row.grad_qkv[0]
 
     def stage_down(row, *earlier):
-        row.inner = [after(x, *earlier) for x in row.inner]
-        row.mlp = scatter_halves(lambda s: dot(row.inner[s], down_full, 1, 1))
+        inner = line.spread([after(x, *earlier) for x in row.inner])
+        low = dot(inner, down_full, 1, 1).astype(BF16)
+        row.mlp = lax.psum_scatter(low, "heads", scatter_dimension=0, tiled=True).astype(F32)
 
     def stage_end(row):
         row.input_grad = row.grad_state + norm_back(
@@ -476,7 +498,7 @@
     first, second = rows
     for row in rows:
         row.ones = gather_halves(row.normed_one)
-        row.grads = gather_halves(row.grad_y)
+        row.grads = line.pick(lax.all_gather(row.grad_y, "heads", axis=0, tiled=True))
     token = stage_attend(first)
     token = stage_attend(second, token)
     token = stage_norm(first, token)

time: 878 us -> 811 us (0.924)
  starting transfers between devices: 289 us -> 192 us
  waiting for transfers between devices: 247 us -> 280 us
  matrix products: 197 us -> 177 us
  local copies, waits for them, and re-layouts: 14.4 us -> 25.2 us
  other arithmetic: 65 us -> 75.7 us
    ppermute x96 -> x72, starting transfers between devices: 242 us -> 157 us  [hop(): return lax.ppermute(value, 'heads', pairs)]
    ppermute x96 -> x72, waiting for transfers between devices: 233 us -> 264 us  [hop(): return lax.ppermute(value, 'heads', pairs)]
    dot_general x60 -> x58, matrix products: 197 us -> 177 us  [dot(): lax.dot_general(a, b, (((ca,), (cb,)), ((), ())), preferred_element_type=...]
    ppermute x23, starting transfers between devices: 43.4 us -> 30.8 us  [shifts(): lax.ppermute(value_of(k), axis, [(i, (i + k) % n) for i in range(n)])]
  transfers between devices with their start and end apart: 143 -> 119, of which waited for: 51 -> 47; matrix products, arithmetic and copies ran while one was open for 29% -> 30% of each run, Pallas kernels for 3% -> 3%
where the time goes in v2:
time: 811 us; the launch traced here: 805 us
  waiting for transfers between devices  280 us (35%)
  starting transfers between devices  192 us (24%)
  matrix products  177 us (22%)
  other arithmetic  75.7 us (9%)
  Pallas kernels  35.8 us (4%)
  local copies, waits for them, and re-layouts  25.2 us (3%)
  between operations  18.1 us (2%)
    ppermute x72, waiting for transfers between devices, hop(): return lax.ppermute(value, 'heads', pairs)  264 us
    dot_general x58, matrix products, dot(): lax.dot_general(a, b, (((ca,), (cb,)), ((), ())), preferred_element_type=...  177 us
    ppermute x72, starting transfers between devices, hop(): return lax.ppermute(value, 'heads', pairs)  157 us
    ppermute x23, starting transfers between devices, shifts(): lax.ppermute(value_of(k), axis, [(i, (i + k) % n) for i in range(n)])  30.8 us
    pallas_call x2, Pallas kernels, attend_back(): pl.pallas_call(functools.partial(backward_kernel, chips, heads), out_shap...  21 us
  transfers between devices with their start and end apart: 119, of which 47 were waited for; matrix products, arithmetic and copies ran while one was open for 30% of the time, Pallas kernels for 3%

profile of v2, /device:TPU:0, one launch (start us, length us, event | category | flops | bytes accessed | tf_op | source)
XLA Modules:
  0.0 804.6 jit_solution(15203017746565622119)
XLA Ops:
  47.0 14.3 %collective-permute-done.24 = bf16[128,2048]{1,0:T(8,128)(2,1)} collective-permute-done((bf16[128,2048]{1,0:T(8,128)(2,1)S(1)}, bf16[128,2048]{1,0:T(8,128)(2,1)}, u32[]{:S(2)}, u32[]{:S(2)}) %collective-permute-start.24) | collective-permute-done | bytes 524320 | tf_op jit(solution)/shard_map/ppermute | solution.py:53
  62.8 8.8 %collective-permute-done.25 = bf16[128,2048]{1,0:T(8,128)(2,1)} collective-permute-done((bf16[128,2048]{1,0:T(8,128)(2,1)S(1)}, bf16[128,2048]{1,0:T(8,128)(2,1)}, u32[]{:S(2)}, u32[]{:S(2)}) %collective-permute-start.25) | collective-permute-done | bytes 524320 | tf_op jit(solution)/shard_map/ppermute | solution.py:53
  72.8 7.3 collective-permute-done.10
  85.1 9.0 %collective-permute-done.26 = bf16[128,2048]{1,0:T(8,128)(2,1)} collective-permute-done((bf16[128,2048]{1,0:T(8,128)(2,1)}, bf16[128,2048]{1,0:T(8,128)(2,1)}, u32[]{:S(2)}, u32[]{:S(2)}) %collective-permute-start.26) | collective-permute-done | bytes 524320 | tf_op jit(solution)/shard_map/ppermute | solution.py:53
  97.2 8.1 %collective-permute-done.12 = bf16[128,2048]{1,0:T(8,128)(2,1)} collective-permute-done((bf16[128,2048]{1,0:T(8,128)(2,1)}, bf16[128,2048]{1,0:T(8,128)(2,1)}, u32[]{:S(2)}, u32[]{:S(2)}) %collective-permute-start.12) | collective-permute-done | bytes 524320 | tf_op jit(solution)/shard_map/ppermute | solution.py:53
  109.5 17.6 %collective-permute-done.13 = bf16[128,2048]{1,0:T(8,128)(2,1)S(1)} collective-permute-done((bf16[128,2048]{1,0:T(8,128)(2,1)}, bf16[128,2048]{1,0:T(8,128)(2,1)S(1)}, u32[]{:S(2)}, u32[]{:S(2)}) %collective-permute-start.13) | collective-permute-done | bytes 524320 | tf_op jit(solution)/shard_map/ppermute | solution.py:53
  147.6 9.7 %attend.3 = (bf16[512,256]{1,0:T(8,128)(2,1)S(1)}, bf16[512,256]{1,0:T(8,128)(2,1)S(1)}, bf16[1024,768]{1,0:T(8,128)(2,1)S(1)}, f32[8,1024]{1,0:T(8,128)S(1)}) custom-call(s32[3]{0:T(128)S(1)} %get-tuple-element.239.where_ref, f32[512,768]{1,0:T(8,128)S(1)} %fusion.107.own_ref, f32[512,768]{1,0:T(8,128)S(1)} %fusion.106.sib_ref, ...), custom_call_target="tpu_custom_call" | custom-call | flops 2147483648 | bytes 8388608 | tf_op jit(solution)/shard_map/attend/pallas_call | solution.py:295
  167.7 14.3 %collective-permute-done.18 = bf16[128,2048]{1,0:T(8,128)(2,1)S(1)} collective-permute-done((bf16[128,2048]{1,0:T(8,128)(2,1)S(1)}, bf16[128,2048]{1,0:T(8,128)(2,1)S(1)}, u32[]{:S(2)}, u32[]{:S(2)}) %collective-permute-start.18) | collective-permute-done | bytes 524320 | tf_op jit(solution)/shard_map/ppermute | solution.py:53
  187.4 5.8 collective-permute-done.38
  207.1 5.8 collective-permute-start.20
  247.0 5.6 collective-permute-start.31
  287.7 7.7 collective-permute-done.33
  299.2 19.8 %collective-permute-done.34 = bf16[128,2048]{1,0:T(8,128)(2,1)S(1)} collective-permute-done((bf16[128,2048]{1,0:T(8,128)(2,1)}, bf16[128,2048]{1,0:T(8,128)(2,1)S(1)}, u32[]{:S(2)}, u32[]{:S(2)}) %collective-permute-start.34) | collective-permute-done | bytes 524320 | tf_op jit(solution)/shard_map/ppermute | solution.py:53
  354.8 5.5 convolution_convert_fusion.1
  390.4 6.1 fusion.66
  444.4 16.6 %collective-permute-done.53 = bf16[128,2048]{1,0:T(8,128)(2,1)S(1)} collective-permute-done((bf16[128,2048]{1,0:T(8,128)(2,1)S(1)}, bf16[128,2048]{1,0:T(8,128)(2,1)S(1)}, u32[]{:S(2)}, u32[]{:S(2)}) %collective-permute-start.53) | collective-permute-done | bytes 524320 | tf_op jit(solution)/shard_map/ppermute | solution.py:53
  468.3 9.1 %collective-permute-done.66 = bf16[128,2048]{1,0:T(8,128)(2,1)S(1)} collective-permute-done((bf16[128,2048]{1,0:T(8,128)(2,1)S(1)}, bf16[128,2048]{1,0:T(8,128)(2,1)S(1)}, u32[]{:S(2)}, u32[]{:S(2)}) %collective-permute-start.66) | collective-permute-done | bytes 524320 | tf_op jit(solution)/shard_map/ppermute | solution.py:53
  491.3 6.2 collective-permute-start.55
  513.6 6.0 collective-permute-done.71
  549.4 9.4 %collective-permute-done.59 = bf16[128,2048]{1,0:T(8,128)(2,1)S(1)} collective-permute-done((bf16[128,2048]{1,0:T(8,128)(2,1)S(1)}, bf16[128,2048]{1,0:T(8,128)(2,1)S(1)}, u32[]{:S(2)}, u32[]{:S(2)}) %collective-permute-start.59) | collective-permute-done | bytes 524320 | tf_op jit(solution)/shard_map/ppermute | solution.py:53
  560.9 6.5 collective-permute-done.60
  570.1 11.8 %collective-permute-done.82 = bf16[128,2048]{1,0:T(8,128)(2,1)S(1)} collective-permute-done((bf16[128,2048]{1,0:T(8,128)(2,1)S(1)}, bf16[128,2048]{1,0:T(8,128)(2,1)S(1)}, u32[]{:S(2)}, u32[]{:S(2)}) %collective-permute-start.82) | collective-permute-done | bytes 524320 | tf_op jit(solution)/shard_map/ppermute | solution.py:53
  583.2 9.9 %collective-permute-done.61 = bf16[128,2048]{1,0:T(8,128)(2,1)S(1)} collective-permute-done((bf16[128,2048]{1,0:T(8,128)(2,1)S(1)}, bf16[128,2048]{1,0:T(8,128)(2,1)S(1)}, u32[]{:S(2)}, u32[]{:S(2)}) %collective-permute-start.61) | collective-permute-done | bytes 524320 | tf_op jit(solution)/shard_map/ppermute | solution.py:53
  594.5 18.0 %collective-permute-done.62 = bf16[128,2048]{1,0:T(8,128)(2,1)S(1)} collective-permute-done((bf16[128,2048]{1,0:T(8,128)(2,1)S(1)}, bf16[128,2048]{1,0:T(8,128)(2,1)S(1)}, u32[]{:S(2)}, u32[]{:S(2)}) %collective-permute-start.62) | collective-permute-done | bytes 524320 | tf_op jit(solution)/shard_map/ppermute | solution.py:53
  632.4 6.9 attend_back.2
  644.5 14.1 %attend_back.3 = (bf16[512,768]{1,0:T(8,128)(2,1)S(1)}, bf16[512,768]{1,0:T(8,128)(2,1)S(1)}, f32[8,768]{1,0:T(8,128)S(1)}) custom-call(s32[3]{0:T(128)S(1)} %copy-done.16, bf16[512,256]{1,0:T(8,128)(2,1)S(1)} %convolution_convert_fusion.7.own_ref, bf16[512,256]{1,0:T(8,128)(2,1)S(1)} %convolution_convert_fusion.6.sib_ref, bf16[1024,768]{1,0:T(8,128)(2,1)S(1)} %copy-done.20, ...), custom_call_target="tpu_custom_call" | custom-call | flops 5368709120 | bytes 8388608 | tf_op jit(solution)/shard_map/attend_back/pallas_call | solution.py:322
  671.5 6.1 fusion.136
  686.0 5.7 add_convert_fusion
  704.7 6.0 collective-permute-done.74
  726.2 6.1 collective-permute-done.75
  741.9 5.4 collective-permute-start.76
  753.8 6.0 collective-permute-start.90
  (785 shorter events, 491.3 us)
Async XLA Ops:
  7.2 245.6 %all-gather.14.cloned.1.call-start = ((), (), s32[]{:S(2)}) async-start(), calls=%async_computation.11 | async-start | bytes 4718592 | tf_op jit(solution)/shard_map/all_gather | solution.py:501
  12.6 257.0 %all-gather.12.cloned.1.call-start = ((), (), s32[]{:S(2)}) async-start(), calls=%async_computation.10 | async-start | bytes 3604480 | tf_op jit(solution)/shard_map/all_gather | solution.py:405
  13.4 262.9 %all-gather.10.cloned.1.call-start = ((), (), s32[]{:S(2)}) async-start(), calls=%async_computation.9 | async-start | bytes 4718592 | tf_op jit(solution)/shard_map/all_gather | solution.py:501
  38.7 32.9 %collective-permute-start.25 = (bf16[128,2048]{1,0:T(8,128)(2,1)S(1)}, bf16[128,2048]{1,0:T(8,128)(2,1)}, u32[]{:S(2)}, u32[]{:S(2)}) collective-permute-start(bf16[128,2048]{1,0:T(8,128)(2,1)S(1)} %get-tuple-element.202), channel_id=1, source_target_pairs={{2,0},{3,1},{4,2},{5,3},{6,4},{7,5},{10,8},{11,9},{12,10},{13,11},... | collective-permute-start | bytes 1572872 | tf_op jit(solution)/shard_map/ppermute | solution.py:53
  39.9 40.2 %collective-permute-start.10 = (bf16[128,2048]{1,0:T(8,128)(2,1)S(1)}, bf16[128,2048]{1,0:T(8,128)(2,1)}, u32[]{:S(2)}, u32[]{:S(2)}) collective-permute-start(bf16[128,2048]{1,0:T(8,128)(2,1)S(1)} %get-tuple-element.201), channel_id=1, source_target_pairs={{0,2},{1,3},{2,4},{3,5},{4,6},{5,7},{8,10},{9,11},{10,12},{11,13},... | collective-permute-start | bytes 1572872 | tf_op jit(solution)/shard_map/ppermute | solution.py:53
  45.3 277.1 %all-gather.6.cloned.1.call-start = ((), (), s32[]{:S(2)}) async-start(), calls=%async_computation.7 | async-start | bytes 3604480 | tf_op jit(solution)/shard_map/all_gather | solution.py:403
  45.4 37.6 %collective-permute-start.11 = (bf16[128,2048]{1,0:T(8,128)(2,1)S(1)}, bf16[128,2048]{1,0:T(8,128)(2,1)}, u32[]{:S(2)}, u32[]{:S(2)}) collective-permute-start(bf16[128,2048]{1,0:T(8,128)(2,1)S(1)} %get-tuple-element.201), channel_id=1, source_target_pairs={{2,0},{3,1},{4,2},{5,3},{6,4},{7,5},{10,8},{11,9},{12,10},{13,11},... | collective-permute-start | bytes 1572872 | tf_op jit(solution)/shard_map/ppermute | solution.py:53
  84.4 43.2 %collective-permute-start.29 = (bf16[128,2048]{1,0:T(8,128)(2,1)}, bf16[128,2048]{1,0:T(8,128)(2,1)S(1)}, u32[]{:S(2)}, u32[]{:S(2)}) collective-permute-start(bf16[128,2048]{1,0:T(8,128)(2,1)} %collective-permute-done.28), channel_id=1, source_target_pairs={{4,6},{5,7},{12,14},{13,15},{20,22},{21,23},{28,30},{29,31}} | collective-permute-start | bytes 1572872 | tf_op jit(solution)/shard_map/ppermute | solution.py:53
  94.0 34.7 %collective-permute-start.27 = (bf16[128,2048]{1,0:T(8,128)(2,1)}, bf16[128,2048]{1,0:T(8,128)(2,1)S(1)}, u32[]{:S(2)}, u32[]{:S(2)}) collective-permute-start(bf16[128,2048]{1,0:T(8,128)(2,1)} %collective-permute-done.26), channel_id=1, source_target_pairs={{2,0},{3,1},{10,8},{11,9},{18,16},{19,17},{26,24},{27,25}} | collective-permute-start | bytes 1572872 | tf_op jit(solution)/shard_map/ppermute | solution.py:53
  164.5 28.8 %collective-permute-start.38 = (bf16[128,2048]{1,0:T(8,128)(2,1)S(1)}, bf16[128,2048]{1,0:T(8,128)(2,1)S(1)}, u32[]{:S(2)}, u32[]{:S(2)}) collective-permute-start(bf16[128,2048]{1,0:T(8,128)(2,1)S(1)} %get-tuple-element.196), channel_id=1, source_target_pairs={{0,2},{1,3},{8,10},{9,11},{16,18},{17,19},{24,26},{25,27}} | collective-permute-start | bytes 1572872 | tf_op jit(solution)/shard_map/ppermute | solution.py:53
  167.0 26.2 %collective-permute-start.41 = (bf16[128,2048]{1,0:T(8,128)(2,1)S(1)}, bf16[128,2048]{1,0:T(8,128)(2,1)S(1)}, u32[]{:S(2)}, u32[]{:S(2)}) collective-permute-start(bf16[128,2048]{1,0:T(8,128)(2,1)S(1)} %get-tuple-element.197), channel_id=1, source_target_pairs={{6,4},{7,5},{14,12},{15,13},{22,20},{23,21},{30,28},{31,29}} | collective-permute-start | bytes 1572872 | tf_op jit(solution)/shard_map/ppermute | solution.py:53
  213.0 114.7 %all-gather.8.cloned.1.call-start = ((), (), s32[]{:S(2)}) async-start(), calls=%async_computation.8 | async-start | bytes 3604480 | tf_op jit(solution)/shard_map/all_gather | solution.py:404
  252.6 271.8 %reduce-scatter.8.cloned.1.call-start = ((), (), s32[]{:S(2)}) async-start(), calls=%async_computation.12 | async-start | bytes 4718592 | tf_op jit(solution)/shard_map/reduce_scatter | solution.py:482
  280.4 40.3 %collective-permute-start.49 = (bf16[128,2048]{1,0:T(8,128)(2,1)}, bf16[128,2048]{1,0:T(8,128)(2,1)S(1)}, u32[]{:S(2)}, u32[]{:S(2)}) collective-permute-start(bf16[128,2048]{1,0:T(8,128)(2,1)} %collective-permute-done.48), channel_id=1, source_target_pairs={{4,6},{5,7},{12,14},{13,15},{20,22},{21,23},{28,30},{29,31}} | collective-permute-start | bytes 1572872 | tf_op jit(solution)/shard_map/ppermute | solution.py:53
  286.2 34.6 %collective-permute-start.47 = (bf16[128,2048]{1,0:T(8,128)(2,1)}, bf16[128,2048]{1,0:T(8,128)(2,1)S(1)}, u32[]{:S(2)}, u32[]{:S(2)}) collective-permute-start(bf16[128,2048]{1,0:T(8,128)(2,1)} %collective-permute-done.46), channel_id=1, source_target_pairs={{2,0},{3,1},{10,8},{11,9},{18,16},{19,17},{26,24},{27,25}} | collective-permute-start | bytes 1572872 | tf_op jit(solution)/shard_map/ppermute | solution.py:53
  360.3 168.2 %reduce-scatter.10.cloned.1.call-start = ((), (), s32[]{:S(2)}) async-start(), calls=%async_computation.13 | async-start | bytes 4718592 | tf_op jit(solution)/shard_map/reduce_scatter | solution.py:482
  378.2 238.3 %reduce-scatter.16.cloned.1.call-start = ((), (), s32[]{:S(2)}) async-start(), calls=%async_computation.16 | async-start | bytes 3604480 | tf_op jit(solution)/shard_map/reduce_scatter | solution.py:524
  390.1 228.8 %reduce-scatter.18.cloned.1.call-start = ((), (), s32[]{:S(2)}) async-start(), calls=%async_computation.17 | async-start | bytes 3604480 | tf_op jit(solution)/shard_map/reduce_scatter | solution.py:524
  411.4 26.8 %collective-permute-start.65 = (bf16[512,2048]{1,0:T(8,128)(2,1)}, bf16[512,2048]{1,0:T(8,128)(2,1)}, u32[]{:S(2)}, u32[]{:S(2)}) collective-permute-start(bf16[512,2048]{1,0:T(8,128)(2,1)} %add_convert_fusion.7), channel_id=1, source_target_pairs={{0,1},{1,0},{2,3},{3,2},{4,5},{5,4},{6,7},{7,6},{8,9},{9,8},{10,11... | collective-permute-start | bytes 6291464 | tf_op jit(solution)/shard_map/ppermute | solution.py:57
  425.4 196.0 %reduce-scatter.20.cloned.1.call-start = ((), (), s32[]{:S(2)}) async-start(), calls=%async_computation.18 | async-start | bytes 3604480 | tf_op jit(solution)/shard_map/reduce_scatter | solution.py:524
  434.4 26.6 %collective-permute-start.53 = (bf16[128,2048]{1,0:T(8,128)(2,1)S(1)}, bf16[128,2048]{1,0:T(8,128)(2,1)S(1)}, u32[]{:S(2)}, u32[]{:S(2)}) collective-permute-start(bf16[128,2048]{1,0:T(8,128)(2,1)S(1)} %get-tuple-element.178), channel_id=1, source_target_pairs={{0,2},{1,3},{8,10},{9,11},{16,18},{17,19},{24,26},{25,27}} | collective-permute-start | bytes 1572872 | tf_op jit(solution)/shard_map/ppermute | solution.py:53
  442.0 35.5 %collective-permute-start.66 = (bf16[128,2048]{1,0:T(8,128)(2,1)S(1)}, bf16[128,2048]{1,0:T(8,128)(2,1)S(1)}, u32[]{:S(2)}, u32[]{:S(2)}) collective-permute-start(bf16[128,2048]{1,0:T(8,128)(2,1)S(1)} %get-tuple-element.184), channel_id=1, source_target_pairs={{0,2},{1,3},{8,10},{9,11},{16,18},{17,19},{24,26},{25,27}} | collective-permute-start | bytes 1572872 | tf_op jit(solution)/shard_map/ppermute | solution.py:53
  443.7 33.8 %collective-permute-start.69 = (bf16[128,2048]{1,0:T(8,128)(2,1)S(1)}, bf16[128,2048]{1,0:T(8,128)(2,1)S(1)}, u32[]{:S(2)}, u32[]{:S(2)}) collective-permute-start(bf16[128,2048]{1,0:T(8,128)(2,1)S(1)} %get-tuple-element.185), channel_id=1, source_target_pairs={{6,4},{7,5},{14,12},{15,13},{22,20},{23,21},{30,28},{31,29}} | collective-permute-start | bytes 1572872 | tf_op jit(solution)/shard_map/ppermute | solution.py:53
  461.3 27.4 %collective-permute-start.54 = (bf16[128,2048]{1,0:T(8,128)(2,1)S(1)}, bf16[128,2048]{1,0:T(8,128)(2,1)S(1)}, u32[]{:S(2)}, u32[]{:S(2)}) collective-permute-start(bf16[128,2048]{1,0:T(8,128)(2,1)S(1)} %get-tuple-element.176), channel_id=1, source_target_pairs={{0,2},{1,3},{2,4},{3,5},{8,10},{9,11},{10,12},{11,13},{16,18},{17,... | collective-permute-start | bytes 1572872 | tf_op jit(solution)/shard_map/ppermute | solution.py:53
  502.3 246.2 %reduce-scatter.14.cloned.1.call-start = ((), (), s32[]{:S(2)}) async-start(), calls=%async_computation.15 | async-start | bytes 1310720 | tf_op jit(solution)/shard_map/reduce_scatter | solution.py:524
  567.3 25.7 %collective-permute-start.61 = (bf16[128,2048]{1,0:T(8,128)(2,1)S(1)}, bf16[128,2048]{1,0:T(8,128)(2,1)S(1)}, u32[]{:S(2)}, u32[]{:S(2)}) collective-permute-start(bf16[128,2048]{1,0:T(8,128)(2,1)S(1)} %collective-permute-done.60), channel_id=1, source_target_pairs={{2,0},{3,1},{4,2},{5,3},{10,8},{11,9},{12,10},{13,11},{18,16},{19,... | collective-permute-start | bytes 1572872 | tf_op jit(solution)/shard_map/ppermute | solution.py:53
  568.6 45.7 %collective-permute-start.85 = (bf16[128,2048]{1,0:T(8,128)(2,1)S(1)}, bf16[128,2048]{1,0:T(8,128)(2,1)S(1)}, u32[]{:S(2)}, u32[]{:S(2)}) collective-permute-start(bf16[128,2048]{1,0:T(8,128)(2,1)S(1)} %collective-permute-done.84), channel_id=1, source_target_pairs={{4,6},{5,7},{12,14},{13,15},{20,22},{21,23},{28,30},{29,31}} | collective-permute-start | bytes 1572872 | tf_op jit(solution)/shard_map/ppermute | solution.py:53
  581.9 32.5 %collective-permute-start.83 = (bf16[128,2048]{1,0:T(8,128)(2,1)S(1)}, bf16[128,2048]{1,0:T(8,128)(2,1)S(1)}, u32[]{:S(2)}, u32[]{:S(2)}) collective-permute-start(bf16[128,2048]{1,0:T(8,128)(2,1)S(1)} %collective-permute-done.82), channel_id=1, source_target_pairs={{2,0},{3,1},{10,8},{11,9},{18,16},{19,17},{26,24},{27,25}} | collective-permute-start | bytes 1572872 | tf_op jit(solution)/shard_map/ppermute | solution.py:53
  616.1 25.9 %collective-permute-start.86 = (bf16[512,2048]{1,0:T(8,128)(2,1)}, bf16[512,2048]{1,0:T(8,128)(2,1)}, u32[]{:S(2)}, u32[]{:S(2)}) collective-permute-start(bf16[512,2048]{1,0:T(8,128)(2,1)} %pad_maximum_fusion.10), channel_id=1, source_target_pairs={{0,1},{1,0},{2,3},{3,2},{4,5},{5,4},{6,7},{7,6},{8,9},{9,8},{10,11... | collective-permute-start | bytes 6291464 | tf_op jit(solution)/shard_map/ppermute | solution.py:57
  661.7 37.4 %collective-permute-start.87 = (bf16[512,2048]{1,0:T(8,128)(2,1)}, bf16[512,2048]{1,0:T(8,128)(2,1)}, u32[]{:S(2)}, u32[]{:S(2)}) collective-permute-start(bf16[512,2048]{1,0:T(8,128)(2,1)} %convolution_convert_fusion.4), channel_id=1, source_target_pairs={{0,1},{1,0},{2,3},{3,2},{4,5},{5,4},{6,7},{7,6},{8,9},{9,8},{10,11... | collective-permute-start | bytes 6291464 | tf_op jit(solution)/shard_map/ppermute | solution.py:57
  664.9 26.8 %collective-permute-start.73 = (bf16[512,2048]{1,0:T(8,128)(2,1)}, bf16[512,2048]{1,0:T(8,128)(2,1)}, u32[]{:S(2)}, u32[]{:S(2)}) collective-permute-start(bf16[512,2048]{1,0:T(8,128)(2,1)} %convolution_convert_fusion.5), channel_id=1, source_target_pairs={{0,1},{1,0},{2,3},{3,2},{4,5},{5,4},{6,7},{7,6},{8,9},{9,8},{10,11... | collective-permute-start | bytes 6291464 | tf_op jit(solution)/shard_map/ppermute | solution.py:57
  671.3 123.5 %reduce-scatter.12.cloned.1.call-start = ((), (), s32[]{:S(2)}) async-start(), calls=%async_computation.14 | async-start | bytes 3932160 | tf_op jit(solution)/shard_map/reduce_scatter | solution.py:524
  (266 other events, 3880.2 us)
Sparse Core Ops, SparseCore 0:
  12.7 65.4 all-gather.13
  80.1 45.9 all-gather.11
  128.2 49.5 all-gather.9
  213.1 42.2 all-gather.5
  257.0 41.6 all-gather.7
  360.5 48.6 reduce-scatter.7
  411.4 68.0 reduce-scatter.9
  482.6 40.1 reduce-scatter.15
  525.9 41.7 reduce-scatter.17
  570.5 41.7 reduce-scatter.19
  671.4 25.9 reduce-scatter.13
  700.5 44.2 reduce-scatter.11

commit v3 on v2

--- a/solution.py
+++ b/solution.py
@@ -107,33 +107,37 @@
     return (a.astype(F32) + b.astype(F32)).astype(BF16)
 
 
-def shifts(value_of, axis):
-    n = lax.axis_size(axis)
-    received = [value_of(0)]
-    for k in range(1, n):
-        received.append(lax.ppermute(value_of(k), axis, [(i, (i + k) % n) for i in range(n)]))
-    return received
-
-
-def small_gather(value, axis):
-    n = lax.axis_size(axis)
-    received = shifts(lambda k: value, axis)
+def ring(axis, group):
+    size, index = lax.axis_size(axis), lax.axis_index(axis)
+    if group == "core":
+        return 2, index % 2, lambda k: [(i, i ^ k) for i in range(size)]
+    if group == "chip":
+        return size // 2, index // 2, lambda k: [(i, (i + 2 * k) % size) for i in range(size)]
+    return size, index, lambda k: [(i, (i + k) % size) for i in range(size)]
+
+
+def shifts(value_of, axis, group):
+    n, _, pairs = ring(axis, group)
+    return [value_of(0)] + [lax.ppermute(value_of(k), axis, pairs(k)) for k in range(1, n)]
+
+
+def small_gather(value, axis, group="all"):
+    n, me, _ = ring(axis, group)
+    received = shifts(lambda k: value, axis, group)
     width = value.shape[1]
     ordered = jnp.concatenate(received[::-1], axis=1)
     doubled = jnp.concatenate([ordered, ordered], axis=1)
-    start = (n - 1 - lax.axis_index(axis)) * width
-    return lax.dynamic_slice_in_dim(doubled, start, n * width, 1)
-
-
-def small_scatter(value, axis, dim):
-    n = lax.axis_size(axis)
+    return lax.dynamic_slice_in_dim(doubled, (n - 1 - me) * width, n * width, 1)
+
+
+def small_scatter(value, axis, dim, group="all"):
+    n, me, _ = ring(axis, group)
     width = value.shape[dim] // n
-    me = lax.axis_index(axis)
 
     def part(k):
         return lax.dynamic_slice_in_dim(value, ((me + k) % n) * width, width, dim)
 
-    return functools.reduce(jnp.add, shifts(part, axis))
+    return functools.reduce(jnp.add, shifts(part, axis, group))
 
 
 def piece_rows(where_ref, s, k, chips, size):
@@ -394,7 +398,7 @@
     tables = rope_tables(seq_full, width)
 
     vectors = jnp.stack([norm1_gain, norm1_bias, norm2_gain, norm2_bias])
-    vectors = small_gather(small_gather(vectors, "heads").reshape(4, -1), "batch")
+    vectors = small_gather(small_gather(small_gather(vectors, "heads", "core"), "heads", "chip"), "batch")
     gain_one, shift_one, gain_two, shift_two = (vectors[i] for i in range(4))
 
     qkv_flat = jnp.concatenate([qkv_weight[:, j] for j in range(3)], axis=1)
@@ -411,6 +415,7 @@
     def scatter_halves(product):
         received = line.swap(product(1).astype(BF16))
         summed = (product(0) + received.astype(F32)).astype(BF16)
+        line.token = summed
         return line.scatter([summed[k * piece : (k + 1) * piece] for k in range(chips)])
 
     class Row:
@@ -505,36 +510,40 @@
     token = stage_norm(second, token)
     token = stage_mlp(first, token)
     token = stage_mlp(second, token)
+    middle = line.token
     stage_down(first, token)
     stage_down(second, token)
     token = stage_state(first, token)
     token = stage_state(second, token)
     token = stage_back(first, token)
     token = stage_back(second, token)
+    last = line.token
     for row in rows:
         stage_end(row)
 
-    def weight_grad(left, right, dim):
+    parts = {}
+
+    def weight_grad(left, right, dim, *earlier):
         total = None
         for row in rows:
             for s in range(2):
-                term = dot(getattr(row, left)[s], getattr(row, right)[s], 0, 0)
+                term = dot(after(getattr(row, left)[s], *earlier), getattr(row, right)[s], 0, 0)
                 total = term if total is None else total + term
-        low = total.astype(BF16)
+        low = parts[left] = total.astype(BF16)
         return lax.psum_scatter(low, "batch", scatter_dimension=dim, tiled=True).astype(F32)
 
-    down_grad = weight_grad("grads", "inner", 0)
-    gate_grad = weight_grad("twos", "grad_gate", 0)
-    up_grad = weight_grad("twos", "grad_up", 0)
-    out_grad_w = weight_grad("attn", "states", 1)
-    qkv_grad = weight_grad("ones", "grad_qkv", 0)
+    down_grad = weight_grad("grads", "inner", 0, middle)
+    gate_grad = weight_grad("twos", "grad_gate", 0, middle)
+    up_grad = weight_grad("twos", "grad_up", 0, middle)
+    out_grad_w = weight_grad("attn", "states", 1, last)
+    qkv_grad = weight_grad("ones", "grad_qkv", 0, last)
     qkv_grad = jnp.stack([qkv_grad[:, j * width : (j + 1) * width] for j in range(3)], axis=1)
 
     bias_sum = functools.reduce(jnp.add, [row.bias_grad for row in rows])
     bias_sum = small_scatter(bias_sum.reshape(3 * heads_here, HD), "batch", 1)
     bias_sum = bias_sum.reshape(3, heads_here, -1)
     norm_sum = functools.reduce(jnp.add, [row.norms for row in rows])
-    norm_sum = small_scatter(small_scatter(norm_sum, "batch", 1), "heads", 1)
+    norm_sum = small_scatter(small_scatter(small_scatter(norm_sum, "batch", 1), "heads", 1, "chip"), "heads", 1, "core")
     return (
         jnp.stack([row.output for row in rows])[:, :, None],
         jnp.stack([row.input_grad.astype(BF16) for row in rows])[:, :, None],

time: 811 us -> 780 us (0.962)
  waiting for transfers between devices: 280 us -> 235 us
  starting transfers between devices: 192 us -> 213 us
  matrix products: 177 us -> 158 us
    ppermute x72, waiting for transfers between devices: 264 us -> 221 us  [hop(): return lax.ppermute(value, 'heads', pairs)]
    dot_general x58, matrix products: 177 us -> 158 us  [dot(): lax.dot_general(a, b, (((ca,), (cb,)), ((), ())), preferred_element_type=...]
    ppermute x23 -> x17, starting transfers between devices: 30.8 us -> 47 us  [shifts(): lax.ppermute(value_of(k), axis, pairs(k))]
  transfers between devices with their start and end apart: 119 -> 113, of which waited for: 47 -> 40; matrix products, arithmetic and copies ran while one was open for 30% -> 30% of each run, Pallas kernels for 3% -> 5%
where the time goes in v3:
time: 780 us; the launch traced here: 773 us
  waiting for transfers between devices  235 us (30%)
  starting transfers between devices  213 us (27%)
  matrix products  158 us (20%)
  other arithmetic  80.7 us (10%)
  Pallas kernels  35.6 us (5%)
  local copies, waits for them, and re-layouts  32.8 us (4%)
  between operations  17.8 us (2%)
    ppermute x72, waiting for transfers between devices, hop(): return lax.ppermute(value, 'heads', pairs)  221 us
    ppermute x72, starting transfers between devices, hop(): return lax.ppermute(value, 'heads', pairs)  163 us
    dot_general x58, matrix products, dot(): lax.dot_general(a, b, (((ca,), (cb,)), ((), ())), preferred_element_type=...  158 us
    ppermute x17, starting transfers between devices, shifts(): lax.ppermute(value_of(k), axis, pairs(k))  47 us
    pallas_call x2, Pallas kernels, attend_back(): pl.pallas_call(functools.partial(backward_kernel, chips, heads), out_shap...  21 us
    convert_element_type x12, other arithmetic, add_low(): return (a.astype(F32) + b.astype(F32)).astype(BF16)  19 us
    unnamed x337, local copies, waits for them, and re-layouts  15.9 us
  transfers between devices with their start and end apart: 113, of which 40 were waited for; matrix products, arithmetic and copies ran while one was open for 30% of the time, Pallas kernels for 5%

profile of v3, /device:TPU:0, one launch (start us, length us, event | category | flops | bytes accessed | tf_op | source)
XLA Modules:
  0.0 772.9 jit_solution(4160113666552075286)
XLA Ops:
  35.4 5.4 collective-permute-start.7
  42.2 5.4 collective-permute-start.21
  47.8 23.8 %collective-permute-done.8 = bf16[128,2048]{1,0:T(8,128)(2,1)} collective-permute-done((bf16[128,2048]{1,0:T(8,128)(2,1)S(1)}, bf16[128,2048]{1,0:T(8,128)(2,1)}, u32[]{:S(2)}, u32[]{:S(2)}) %collective-permute-start.8) | collective-permute-done | bytes 524320 | tf_op jit(solution)/shard_map/ppermute | solution.py:53
  75.8 7.1 collective-permute-done.22
  85.7 8.4 %collective-permute-done.9 = bf16[128,2048]{1,0:T(8,128)(2,1)} collective-permute-done((bf16[128,2048]{1,0:T(8,128)(2,1)}, bf16[128,2048]{1,0:T(8,128)(2,1)}, u32[]{:S(2)}, u32[]{:S(2)}) %collective-permute-start.9) | collective-permute-done | bytes 524320 | tf_op jit(solution)/shard_map/ppermute | solution.py:53
  97.3 8.1 %collective-permute-done.23 = bf16[128,2048]{1,0:T(8,128)(2,1)} collective-permute-done((bf16[128,2048]{1,0:T(8,128)(2,1)}, bf16[128,2048]{1,0:T(8,128)(2,1)}, u32[]{:S(2)}, u32[]{:S(2)}) %collective-permute-start.23) | collective-permute-done | bytes 524320 | tf_op jit(solution)/shard_map/ppermute | solution.py:53
  108.8 7.7 collective-permute-done.10
  118.0 9.0 %collective-permute-done.24 = bf16[128,2048]{1,0:T(8,128)(2,1)S(1)} collective-permute-done((bf16[128,2048]{1,0:T(8,128)(2,1)}, bf16[128,2048]{1,0:T(8,128)(2,1)S(1)}, u32[]{:S(2)}, u32[]{:S(2)}) %collective-permute-start.24) | collective-permute-done | bytes 524320 | tf_op jit(solution)/shard_map/ppermute | solution.py:53
  146.7 9.2 %attend.3 = (bf16[512,256]{1,0:T(8,128)(2,1)S(1)}, bf16[512,256]{1,0:T(8,128)(2,1)S(1)}, bf16[1024,768]{1,0:T(8,128)(2,1)S(1)}, f32[8,1024]{1,0:T(8,128)S(1)}) custom-call(s32[3]{0:T(128)S(1)} %get-tuple-element.267.where_ref, f32[512,768]{1,0:T(8,128)S(1)} %fusion.96.own_ref, f32[512,768]{1,0:T(8,128)S(1)} %fusion.95.sib_ref, ...), custom_call_target="tpu_custom_call" | custom-call | flops 2147483648 | bytes 8388608 | tf_op jit(solution)/shard_map/attend/pallas_call | solution.py:299
  165.1 18.0 %collective-permute-done.15 = bf16[128,2048]{1,0:T(8,128)(2,1)S(1)} collective-permute-done((bf16[128,2048]{1,0:T(8,128)(2,1)S(1)}, bf16[128,2048]{1,0:T(8,128)(2,1)S(1)}, u32[]{:S(2)}, u32[]{:S(2)}) %collective-permute-start.15) | collective-permute-done | bytes 524320 | tf_op jit(solution)/shard_map/ppermute | solution.py:53
  233.7 6.0 collective-permute-start.28
  246.0 5.4 collective-permute-start.41
  278.6 8.0 %collective-permute-done.43 = bf16[128,2048]{1,0:T(8,128)(2,1)} collective-permute-done((bf16[128,2048]{1,0:T(8,128)(2,1)}, bf16[128,2048]{1,0:T(8,128)(2,1)}, u32[]{:S(2)}, u32[]{:S(2)}) %collective-permute-start.43) | collective-permute-done | bytes 524320 | tf_op jit(solution)/shard_map/ppermute | solution.py:53
  289.9 7.8 %collective-permute-done.31 = bf16[128,2048]{1,0:T(8,128)(2,1)S(1)} collective-permute-done((bf16[128,2048]{1,0:T(8,128)(2,1)}, bf16[128,2048]{1,0:T(8,128)(2,1)S(1)}, u32[]{:S(2)}, u32[]{:S(2)}) %collective-permute-start.31) | collective-permute-done | bytes 524320 | tf_op jit(solution)/shard_map/ppermute | solution.py:53
  300.5 7.5 collective-permute-done.44
  342.6 5.5 convolution_convert_fusion.1
  407.1 5.6 add_convert_fusion.8
  423.4 27.2 %collective-permute-done.50 = bf16[128,2048]{1,0:T(8,128)(2,1)S(1)} collective-permute-done((bf16[128,2048]{1,0:T(8,128)(2,1)S(1)}, bf16[128,2048]{1,0:T(8,128)(2,1)S(1)}, u32[]{:S(2)}, u32[]{:S(2)}) %collective-permute-start.50) | collective-permute-done | bytes 524320 | tf_op jit(solution)/shard_map/ppermute | solution.py:53
  471.3 6.6 collective-permute-done.51
  487.1 5.7 fusion.130
  503.3 7.5 collective-permute-done.65
  543.1 8.3 %collective-permute-done.57 = bf16[128,2048]{1,0:T(8,128)(2,1)S(1)} collective-permute-done((bf16[128,2048]{1,0:T(8,128)(2,1)S(1)}, bf16[128,2048]{1,0:T(8,128)(2,1)S(1)}, u32[]{:S(2)}, u32[]{:S(2)}) %collective-permute-start.57) | collective-permute-done | bytes 524320 | tf_op jit(solution)/shard_map/ppermute | solution.py:53
  564.0 9.9 %collective-permute-done.58 = bf16[128,2048]{1,0:T(8,128)(2,1)} collective-permute-done((bf16[128,2048]{1,0:T(8,128)(2,1)S(1)}, bf16[128,2048]{1,0:T(8,128)(2,1)}, u32[]{:S(2)}, u32[]{:S(2)}) %collective-permute-start.58) | collective-permute-done | bytes 524320 | tf_op jit(solution)/shard_map/ppermute | solution.py:53
  579.2 13.4 %collective-permute-done.59 = bf16[128,2048]{1,0:T(8,128)(2,1)S(1)} collective-permute-done((bf16[128,2048]{1,0:T(8,128)(2,1)}, bf16[128,2048]{1,0:T(8,128)(2,1)S(1)}, u32[]{:S(2)}, u32[]{:S(2)}) %collective-permute-start.59) | collective-permute-done | bytes 524320 | tf_op jit(solution)/shard_map/ppermute | solution.py:53
  600.2 6.8 attend_back.2
  609.3 14.2 %attend_back.3 = (bf16[512,768]{1,0:T(8,128)(2,1)S(1)}, bf16[512,768]{1,0:T(8,128)(2,1)S(1)}, f32[8,768]{1,0:T(8,128)S(1)}) custom-call(s32[3]{0:T(128)S(1)} %copy-done.18, bf16[512,256]{1,0:T(8,128)(2,1)S(1)} %convolution_convert_fusion.7.own_ref, bf16[512,256]{1,0:T(8,128)(2,1)S(1)} %convolution_convert_fusion.6.sib_ref, bf16[1024,768]{1,0:T(8,128)(2,1)S(1)} %copy-done.24, ...), custom_call_target="tpu_custom_call" | custom-call | flops 5368709120 | bytes 8388608 | tf_op jit(solution)/shard_map/attend_back/pallas_call | solution.py:326
  638.9 6.1 add_convert_fusion.4
  680.2 8.6 %collective-permute-start.98 = (f32[12,16]{1,0:T(8,128)S(1)}, f32[12,16]{1,0:T(8,128)S(1)}, u32[]{:S(2)}, u32[]{:S(2)}) collective-permute-start(f32[12,16]{1,0:T(8,128)S(1)} %get-tuple-element.247), channel_id=1, source_target_pairs={{0,8},{8,16},{16,24},{24,0},{1,9},{9,17},{17,25},{25,1},{2,10},{10... | collective-permute-start | bytes 2312 | tf_op jit(solution)/shard_map/ppermute | solution.py:121
  690.5 7.7 collective-permute-start.99
  715.6 8.1 %collective-permute-start.87 = (bf16[128,2048]{1,0:T(8,128)(2,1)S(1)}, bf16[128,2048]{1,0:T(8,128)(2,1)S(1)}, u32[]{:S(2)}, u32[]{:S(2)}) collective-permute-start(bf16[128,2048]{1,0:T(8,128)(2,1)S(1)} %get-tuple-element.200), channel_id=1, source_target_pairs={{0,2},{1,3},{2,4},{3,5},{4,6},{5,7},{8,10},{9,11},{10,12},{11,13},... | collective-permute-start | bytes 1572872 | tf_op jit(solution)/shard_map/ppermute | solution.py:53
  727.2 8.7 %collective-permute-done.87 = bf16[128,2048]{1,0:T(8,128)(2,1)S(1)} collective-permute-done((bf16[128,2048]{1,0:T(8,128)(2,1)S(1)}, bf16[128,2048]{1,0:T(8,128)(2,1)S(1)}, u32[]{:S(2)}, u32[]{:S(2)}) %collective-permute-start.87) | collective-permute-done | bytes 524320 | tf_op jit(solution)/shard_map/ppermute | solution.py:53
  737.2 8.8 %collective-permute-start.91 = (f32[4,512]{1,0:T(4,128)S(1)}, f32[4,512]{1,0:T(4,128)S(1)}, u32[]{:S(2)}, u32[]{:S(2)}) collective-permute-start(f32[4,512]{1,0:T(4,128)S(1)} %get-tuple-element.244), channel_id=1, source_target_pairs={{0,8},{8,16},{16,24},{24,0},{1,9},{9,17},{17,25},{25,1},{2,10},{10... | collective-permute-start | bytes 24584 | tf_op jit(solution)/shard_map/ppermute | solution.py:121
  (752 shorter events, 459.5 us)
Async XLA Ops:
  7.2 218.7 %all-gather.14.cloned.1.call-start = ((), (), s32[]{:S(2)}) async-start(), calls=%async_computation.11 | async-start | bytes 4718592 | tf_op jit(solution)/shard_map/all_gather | solution.py:506
  12.6 243.1 %all-gather.12.cloned.1.call-start = ((), (), s32[]{:S(2)}) async-start(), calls=%async_computation.10 | async-start | bytes 3604480 | tf_op jit(solution)/shard_map/all_gather | solution.py:409
  13.4 253.5 %all-gather.10.cloned.1.call-start = ((), (), s32[]{:S(2)}) async-start(), calls=%async_computation.9 | async-start | bytes 4718592 | tf_op jit(solution)/shard_map/all_gather | solution.py:506
  14.1 296.6 %all-gather.8.cloned.1.call-start = ((), (), s32[]{:S(2)}) async-start(), calls=%async_computation.8 | async-start | bytes 3604480 | tf_op jit(solution)/shard_map/all_gather | solution.py:408
  34.1 37.6 %collective-permute-start.8 = (bf16[128,2048]{1,0:T(8,128)(2,1)S(1)}, bf16[128,2048]{1,0:T(8,128)(2,1)}, u32[]{:S(2)}, u32[]{:S(2)}) collective-permute-start(bf16[128,2048]{1,0:T(8,128)(2,1)S(1)} %get-tuple-element.233), channel_id=1, source_target_pairs={{2,0},{3,1},{4,2},{5,3},{6,4},{7,5},{10,8},{11,9},{12,10},{13,11},... | collective-permute-start | bytes 1572872 | tf_op jit(solution)/shard_map/ppermute | solution.py:53
  35.4 37.6 %collective-permute-start.7 = (bf16[128,2048]{1,0:T(8,128)(2,1)S(1)}, bf16[128,2048]{1,0:T(8,128)(2,1)}, u32[]{:S(2)}, u32[]{:S(2)}) collective-permute-start(bf16[128,2048]{1,0:T(8,128)(2,1)S(1)} %get-tuple-element.233), channel_id=1, source_target_pairs={{0,2},{1,3},{2,4},{3,5},{4,6},{5,7},{8,10},{9,11},{10,12},{11,13},... | collective-permute-start | bytes 1572872 | tf_op jit(solution)/shard_map/ppermute | solution.py:53
  40.8 275.1 %all-gather.6.cloned.1.call-start = ((), (), s32[]{:S(2)}) async-start(), calls=%async_computation.7 | async-start | bytes 3604480 | tf_op jit(solution)/shard_map/all_gather | solution.py:407
  40.9 42.0 %collective-permute-start.22 = (bf16[128,2048]{1,0:T(8,128)(2,1)S(1)}, bf16[128,2048]{1,0:T(8,128)(2,1)}, u32[]{:S(2)}, u32[]{:S(2)}) collective-permute-start(bf16[128,2048]{1,0:T(8,128)(2,1)S(1)} %get-tuple-element.234), channel_id=1, source_target_pairs={{2,0},{3,1},{4,2},{5,3},{6,4},{7,5},{10,8},{11,9},{12,10},{13,11},... | collective-permute-start | bytes 1572872 | tf_op jit(solution)/shard_map/ppermute | solution.py:53
  42.2 42.0 %collective-permute-start.21 = (bf16[128,2048]{1,0:T(8,128)(2,1)S(1)}, bf16[128,2048]{1,0:T(8,128)(2,1)}, u32[]{:S(2)}, u32[]{:S(2)}) collective-permute-start(bf16[128,2048]{1,0:T(8,128)(2,1)S(1)} %get-tuple-element.234), channel_id=1, source_target_pairs={{0,2},{1,3},{2,4},{3,5},{4,6},{5,7},{8,10},{9,11},{10,12},{11,13},... | collective-permute-start | bytes 1572872 | tf_op jit(solution)/shard_map/ppermute | solution.py:53
  157.6 25.5 %collective-permute-start.15 = (bf16[128,2048]{1,0:T(8,128)(2,1)S(1)}, bf16[128,2048]{1,0:T(8,128)(2,1)S(1)}, u32[]{:S(2)}, u32[]{:S(2)}) collective-permute-start(bf16[128,2048]{1,0:T(8,128)(2,1)S(1)} %get-tuple-element.222), channel_id=1, source_target_pairs={{0,2},{1,3},{8,10},{9,11},{16,18},{17,19},{24,26},{25,27}} | collective-permute-start | bytes 1572872 | tf_op jit(solution)/shard_map/ppermute | solution.py:53
  161.8 32.5 %collective-permute-start.35 = (bf16[128,2048]{1,0:T(8,128)(2,1)S(1)}, bf16[128,2048]{1,0:T(8,128)(2,1)S(1)}, u32[]{:S(2)}, u32[]{:S(2)}) collective-permute-start(bf16[128,2048]{1,0:T(8,128)(2,1)S(1)} %get-tuple-element.228), channel_id=1, source_target_pairs={{0,2},{1,3},{8,10},{9,11},{16,18},{17,19},{24,26},{25,27}} | collective-permute-start | bytes 1572872 | tf_op jit(solution)/shard_map/ppermute | solution.py:53
  164.4 29.9 %collective-permute-start.38 = (bf16[128,2048]{1,0:T(8,128)(2,1)S(1)}, bf16[128,2048]{1,0:T(8,128)(2,1)S(1)}, u32[]{:S(2)}, u32[]{:S(2)}) collective-permute-start(bf16[128,2048]{1,0:T(8,128)(2,1)S(1)} %get-tuple-element.229), channel_id=1, source_target_pairs={{6,4},{7,5},{14,12},{15,13},{22,20},{23,21},{30,28},{31,29}} | collective-permute-start | bytes 1572872 | tf_op jit(solution)/shard_map/ppermute | solution.py:53
  202.1 313.3 %reduce-scatter.8.cloned.1.call-start = ((), (), s32[]{:S(2)}) async-start(), calls=%async_computation.12 | async-start | bytes 4718592 | tf_op jit(solution)/shard_map/reduce_scatter | solution.py:487
  300.5 32.7 %collective-permute-start.47 = (bf16[512,2048]{1,0:T(8,128)(2,1)}, bf16[512,2048]{1,0:T(8,128)(2,1)}, u32[]{:S(2)}, u32[]{:S(2)}) collective-permute-start(bf16[512,2048]{1,0:T(8,128)(2,1)} %pad_maximum_fusion.3), channel_id=1, source_target_pairs={{0,1},{1,0},{2,3},{3,2},{4,5},{5,4},{6,7},{7,6},{8,9},{9,8},{10,11... | collective-permute-start | bytes 6291464 | tf_op jit(solution)/shard_map/ppermute | solution.py:57
  348.1 171.4 %reduce-scatter.10.cloned.1.call-start = ((), (), s32[]{:S(2)}) async-start(), calls=%async_computation.13 | async-start | bytes 4718592 | tf_op jit(solution)/shard_map/reduce_scatter | solution.py:487
  365.9 264.5 %reduce-scatter.20.cloned.1.call-start = ((), (), s32[]{:S(2)}) async-start(), calls=%async_computation.18 | async-start | bytes 3604480 | tf_op jit(solution)/shard_map/reduce_scatter | solution.py:533
  400.2 232.7 %reduce-scatter.18.cloned.1.call-start = ((), (), s32[]{:S(2)}) async-start(), calls=%async_computation.17 | async-start | bytes 3604480 | tf_op jit(solution)/shard_map/reduce_scatter | solution.py:533
  402.6 59.8 %collective-permute-start.63 = (bf16[128,2048]{1,0:T(8,128)(2,1)}, bf16[128,2048]{1,0:T(8,128)(2,1)}, u32[]{:S(2)}, u32[]{:S(2)}) collective-permute-start(bf16[128,2048]{1,0:T(8,128)(2,1)} %get-tuple-element.216), channel_id=1, source_target_pairs={{0,2},{1,3},{8,10},{9,11},{16,18},{17,19},{24,26},{25,27}} | collective-permute-start | bytes 1572872 | tf_op jit(solution)/shard_map/ppermute | solution.py:53
  405.6 56.8 %collective-permute-start.66 = (bf16[128,2048]{1,0:T(8,128)(2,1)}, bf16[128,2048]{1,0:T(8,128)(2,1)}, u32[]{:S(2)}, u32[]{:S(2)}) collective-permute-start(bf16[128,2048]{1,0:T(8,128)(2,1)} %get-tuple-element.217), channel_id=1, source_target_pairs={{6,4},{7,5},{14,12},{15,13},{22,20},{23,21},{30,28},{31,29}} | collective-permute-start | bytes 1572872 | tf_op jit(solution)/shard_map/ppermute | solution.py:53
  412.8 37.8 %collective-permute-start.50 = (bf16[128,2048]{1,0:T(8,128)(2,1)S(1)}, bf16[128,2048]{1,0:T(8,128)(2,1)S(1)}, u32[]{:S(2)}, u32[]{:S(2)}) collective-permute-start(bf16[128,2048]{1,0:T(8,128)(2,1)S(1)} %get-tuple-element.210), channel_id=1, source_target_pairs={{0,2},{1,3},{8,10},{9,11},{16,18},{17,19},{24,26},{25,27}} | collective-permute-start | bytes 1572872 | tf_op jit(solution)/shard_map/ppermute | solution.py:53
  414.2 36.4 %collective-permute-start.53 = (bf16[128,2048]{1,0:T(8,128)(2,1)S(1)}, bf16[128,2048]{1,0:T(8,128)(2,1)S(1)}, u32[]{:S(2)}, u32[]{:S(2)}) collective-permute-start(bf16[128,2048]{1,0:T(8,128)(2,1)S(1)} %get-tuple-element.211), channel_id=1, source_target_pairs={{6,4},{7,5},{14,12},{15,13},{22,20},{23,21},{30,28},{31,29}} | collective-permute-start | bytes 1572872 | tf_op jit(solution)/shard_map/ppermute | solution.py:53
  451.9 26.0 %collective-permute-start.51 = (bf16[128,2048]{1,0:T(8,128)(2,1)}, bf16[128,2048]{1,0:T(8,128)(2,1)}, u32[]{:S(2)}, u32[]{:S(2)}) collective-permute-start(bf16[128,2048]{1,0:T(8,128)(2,1)} %get-tuple-element.208), channel_id=1, source_target_pairs={{0,2},{1,3},{2,4},{3,5},{8,10},{9,11},{10,12},{11,13},{16,18},{17,... | collective-permute-start | bytes 1572872 | tf_op jit(solution)/shard_map/ppermute | solution.py:53
  465.2 27.7 %collective-permute-start.64 = (bf16[128,2048]{1,0:T(8,128)(2,1)}, bf16[128,2048]{1,0:T(8,128)(2,1)}, u32[]{:S(2)}, u32[]{:S(2)}) collective-permute-start(bf16[128,2048]{1,0:T(8,128)(2,1)} %get-tuple-element.214), channel_id=1, source_target_pairs={{0,2},{1,3},{2,4},{3,5},{8,10},{9,11},{10,12},{11,13},{16,18},{17,... | collective-permute-start | bytes 1572872 | tf_op jit(solution)/shard_map/ppermute | solution.py:53
  492.8 142.4 %reduce-scatter.16.cloned.1.call-start = ((), (), s32[]{:S(2)}) async-start(), calls=%async_computation.16 | async-start | bytes 3604480 | tf_op jit(solution)/shard_map/reduce_scatter | solution.py:533
  542.4 33.0 %collective-permute-start.81 = (bf16[128,2048]{1,0:T(8,128)(2,1)S(1)}, bf16[128,2048]{1,0:T(8,128)(2,1)S(1)}, u32[]{:S(2)}, u32[]{:S(2)}) collective-permute-start(bf16[128,2048]{1,0:T(8,128)(2,1)S(1)} %collective-permute-done.77), channel_id=1, source_target_pairs={{2,4},{3,5},{4,6},{5,7},{10,12},{11,13},{12,14},{13,15},{18,20},{1... | collective-permute-start | bytes 1572872 | tf_op jit(solution)/shard_map/ppermute | solution.py:53
  552.7 24.7 %collective-permute-start.60 = (bf16[128,2048]{1,0:T(8,128)(2,1)}, bf16[128,2048]{1,0:T(8,128)(2,1)}, u32[]{:S(2)}, u32[]{:S(2)}) collective-permute-start(bf16[128,2048]{1,0:T(8,128)(2,1)} %collective-permute-done.56), channel_id=1, source_target_pairs={{2,4},{3,5},{4,6},{5,7},{10,12},{11,13},{12,14},{13,15},{18,20},{1... | collective-permute-start | bytes 1572872 | tf_op jit(solution)/shard_map/ppermute | solution.py:53
  557.6 203.8 %reduce-scatter.14.cloned.1.call-start = ((), (), s32[]{:S(2)}) async-start(), calls=%async_computation.15 | async-start | bytes 1310720 | tf_op jit(solution)/shard_map/reduce_scatter | solution.py:533
  562.7 32.0 %collective-permute-start.80 = (bf16[128,2048]{1,0:T(8,128)(2,1)}, bf16[128,2048]{1,0:T(8,128)(2,1)S(1)}, u32[]{:S(2)}, u32[]{:S(2)}) collective-permute-start(bf16[128,2048]{1,0:T(8,128)(2,1)} %collective-permute-done.79), channel_id=1, source_target_pairs={{2,0},{3,1},{10,8},{11,9},{18,16},{19,17},{26,24},{27,25}} | collective-permute-start | bytes 1572872 | tf_op jit(solution)/shard_map/ppermute | solution.py:53
  649.7 26.9 %collective-permute-start.71 = (bf16[128,2048]{1,0:T(8,128)(2,1)}, bf16[128,2048]{1,0:T(8,128)(2,1)}, u32[]{:S(2)}, u32[]{:S(2)}) collective-permute-start(bf16[128,2048]{1,0:T(8,128)(2,1)} %get-tuple-element.198), channel_id=1, source_target_pairs={{0,2},{1,3},{8,10},{9,11},{16,18},{17,19},{24,26},{25,27}} | collective-permute-start | bytes 1572872 | tf_op jit(solution)/shard_map/ppermute | solution.py:53
  660.7 102.5 %reduce-scatter.12.cloned.1.call-start = ((), (), s32[]{:S(2)}) async-start(), calls=%async_computation.14 | async-start | bytes 3932160 | tf_op jit(solution)/shard_map/reduce_scatter | solution.py:533
  679.4 23.5 %collective-permute-start.75 = (bf16[128,2048]{1,0:T(8,128)(2,1)S(1)}, bf16[128,2048]{1,0:T(8,128)(2,1)S(1)}, u32[]{:S(2)}, u32[]{:S(2)}) collective-permute-start(bf16[128,2048]{1,0:T(8,128)(2,1)S(1)} %get-tuple-element.197), channel_id=1, source_target_pairs={{4,2},{5,3},{6,4},{7,5},{12,10},{13,11},{14,12},{15,13},{20,18},{2... | collective-permute-start | bytes 1572872 | tf_op jit(solution)/shard_map/ppermute | solution.py:53
  680.2 23.9 %collective-permute-start.98 = (f32[12,16]{1,0:T(8,128)S(1)}, f32[12,16]{1,0:T(8,128)S(1)}, u32[]{:S(2)}, u32[]{:S(2)}) collective-permute-start(f32[12,16]{1,0:T(8,128)S(1)} %get-tuple-element.247), channel_id=1, source_target_pairs={{0,8},{8,16},{16,24},{24,0},{1,9},{9,17},{17,25},{25,1},{2,10},{10... | collective-permute-start | bytes 2312 | tf_op jit(solution)/shard_map/ppermute | solution.py:121
  (243 other events, 3016.3 us)
Sparse Core Ops, SparseCore 0:
  12.7 64.0 all-gather.13
  78.6 48.5 all-gather.11
  129.4 53.1 all-gather.9
  184.3 46.5 all-gather.7
  232.6 41.6 all-gather.5
  348.2 49.5 reduce-scatter.7
  400.1 78.2 reduce-scatter.9
  481.4 42.4 reduce-scatter.19
  527.0 41.7 reduce-scatter.17
  571.7 41.7 reduce-scatter.15
  660.8 34.8 reduce-scatter.13
  698.8 44.0 reduce-scatter.11

commit v4 on v3

--- a/solution.py
+++ b/solution.py
@@ -513,7 +513,7 @@
     middle = line.token
     stage_down(first, token)
     stage_down(second, token)
-    token = stage_state(first, token)
+    token = stage_state(first)
     token = stage_state(second, token)
     token = stage_back(first, token)
     token = stage_back(second, token)

time: 780 us -> 774 us (level)
  starting transfers between devices: 213 us -> 195 us
  waiting for transfers between devices: 235 us -> 250 us
    ppermute x17, starting transfers between devices: 47 us -> 31.3 us  [shifts(): lax.ppermute(value_of(k), axis, pairs(k))]
    ppermute x72, waiting for transfers between devices: 221 us -> 234 us  [hop(): return lax.ppermute(value, 'heads', pairs)]
    unnamed x337 -> x339, local copies, waits for them, and re-layouts: 15.9 us -> 15.9 us
  transfers between devices with their start and end apart: 113 -> 113, of which waited for: 40 -> 42; matrix products, arithmetic and copies ran while one was open for 30% -> 30% of each run, Pallas kernels for 5% -> 5%
where the time goes in v4:
time: 774 us; the launch traced here: 769 us
  waiting for transfers between devices  250 us (32%)
  starting transfers between devices  195 us (25%)
  matrix products  158 us (20%)
  other arithmetic  80.7 us (10%)
  Pallas kernels  35.2 us (5%)
  local copies, waits for them, and re-layouts  32.8 us (4%)
  between operations  17.8 us (2%)
    ppermute x72, waiting for transfers between devices, hop(): return lax.ppermute(value, 'heads', pairs)  234 us
    ppermute x72, starting transfers between devices, hop(): return lax.ppermute(value, 'heads', pairs)  160 us
    dot_general x58, matrix products, dot(): lax.dot_general(a, b, (((ca,), (cb,)), ((), ())), preferred_element_type=...  158 us
    ppermute x17, starting transfers between devices, shifts(): lax.ppermute(value_of(k), axis, pairs(k))  31.3 us
    pallas_call x2, Pallas kernels, attend_back(): pl.pallas_call(functools.partial(backward_kernel, chips, heads), out_shap...  20.7 us
    convert_element_type x12, other arithmetic, add_low(): return (a.astype(F32) + b.astype(F32)).astype(BF16)  19 us
    unnamed x339, local copies, waits for them, and re-layouts  15.9 us
  transfers between devices with their start and end apart: 113, of which 42 were waited for; matrix products, arithmetic and copies ran while one was open for 30% of the time, Pallas kernels for 5%

profile of v4, /device:TPU:0, one launch (start us, length us, event | category | flops | bytes accessed | tf_op | source)
XLA Modules:
  0.0 768.9 jit_solution(13058141179095100447)
XLA Ops:
  35.4 5.4 collective-permute-start.7
  42.2 5.4 collective-permute-start.21
  47.8 23.9 %collective-permute-done.8 = bf16[128,2048]{1,0:T(8,128)(2,1)} collective-permute-done((bf16[128,2048]{1,0:T(8,128)(2,1)S(1)}, bf16[128,2048]{1,0:T(8,128)(2,1)}, u32[]{:S(2)}, u32[]{:S(2)}) %collective-permute-start.8) | collective-permute-done | bytes 524320 | tf_op jit(solution)/shard_map/ppermute | solution.py:53
  75.8 7.1 collective-permute-done.22
  85.7 8.4 %collective-permute-done.9 = bf16[128,2048]{1,0:T(8,128)(2,1)} collective-permute-done((bf16[128,2048]{1,0:T(8,128)(2,1)}, bf16[128,2048]{1,0:T(8,128)(2,1)}, u32[]{:S(2)}, u32[]{:S(2)}) %collective-permute-start.9) | collective-permute-done | bytes 524320 | tf_op jit(solution)/shard_map/ppermute | solution.py:53
  97.3 8.1 %collective-permute-done.23 = bf16[128,2048]{1,0:T(8,128)(2,1)} collective-permute-done((bf16[128,2048]{1,0:T(8,128)(2,1)}, bf16[128,2048]{1,0:T(8,128)(2,1)}, u32[]{:S(2)}, u32[]{:S(2)}) %collective-permute-start.23) | collective-permute-done | bytes 524320 | tf_op jit(solution)/shard_map/ppermute | solution.py:53
  108.8 7.7 %collective-permute-done.10 = bf16[128,2048]{1,0:T(8,128)(2,1)S(1)} collective-permute-done((bf16[128,2048]{1,0:T(8,128)(2,1)}, bf16[128,2048]{1,0:T(8,128)(2,1)S(1)}, u32[]{:S(2)}, u32[]{:S(2)}) %collective-permute-start.10) | collective-permute-done | bytes 524320 | tf_op jit(solution)/shard_map/ppermute | solution.py:53
  118.0 9.0 %collective-permute-done.24 = bf16[128,2048]{1,0:T(8,128)(2,1)S(1)} collective-permute-done((bf16[128,2048]{1,0:T(8,128)(2,1)}, bf16[128,2048]{1,0:T(8,128)(2,1)S(1)}, u32[]{:S(2)}, u32[]{:S(2)}) %collective-permute-start.24) | collective-permute-done | bytes 524320 | tf_op jit(solution)/shard_map/ppermute | solution.py:53
  136.4 9.6 %attend.2 = (bf16[512,256]{1,0:T(8,128)(2,1)S(1)}, bf16[512,256]{1,0:T(8,128)(2,1)S(1)}, bf16[1024,768]{1,0:T(8,128)(2,1)S(1)}, f32[8,1024]{1,0:T(8,128)S(1)}) custom-call(s32[3]{0:T(128)S(1)} %get-tuple-element.264.where_ref, f32[512,768]{1,0:T(8,128)S(1)} %fusion.98.own_ref, f32[512,768]{1,0:T(8,128)S(1)} %fusion.97.sib_ref, ...), custom_call_target="tpu_custom_call" | custom-call | flops 2147483648 | bytes 8388608 | tf_op jit(solution)/shard_map/attend/pallas_call | solution.py:299
  165.1 18.0 %collective-permute-done.15 = bf16[128,2048]{1,0:T(8,128)(2,1)S(1)} collective-permute-done((bf16[128,2048]{1,0:T(8,128)(2,1)S(1)}, bf16[128,2048]{1,0:T(8,128)(2,1)S(1)}, u32[]{:S(2)}, u32[]{:S(2)}) %collective-permute-start.15) | collective-permute-done | bytes 524320 | tf_op jit(solution)/shard_map/ppermute | solution.py:53
  233.7 6.0 collective-permute-start.28
  246.0 5.4 collective-permute-start.41
  278.6 8.0 %collective-permute-done.43 = bf16[128,2048]{1,0:T(8,128)(2,1)} collective-permute-done((bf16[128,2048]{1,0:T(8,128)(2,1)}, bf16[128,2048]{1,0:T(8,128)(2,1)}, u32[]{:S(2)}, u32[]{:S(2)}) %collective-permute-start.43) | collective-permute-done | bytes 524320 | tf_op jit(solution)/shard_map/ppermute | solution.py:53
  289.9 7.8 %collective-permute-done.31 = bf16[128,2048]{1,0:T(8,128)(2,1)S(1)} collective-permute-done((bf16[128,2048]{1,0:T(8,128)(2,1)}, bf16[128,2048]{1,0:T(8,128)(2,1)S(1)}, u32[]{:S(2)}, u32[]{:S(2)}) %collective-permute-start.31) | collective-permute-done | bytes 524320 | tf_op jit(solution)/shard_map/ppermute | solution.py:53
  300.5 7.5 collective-permute-done.44
  342.6 5.5 convolution_convert_fusion.1
  407.0 5.6 add_convert_fusion.8
  423.5 27.0 %collective-permute-done.50 = bf16[128,2048]{1,0:T(8,128)(2,1)S(1)} collective-permute-done((bf16[128,2048]{1,0:T(8,128)(2,1)S(1)}, bf16[128,2048]{1,0:T(8,128)(2,1)S(1)}, u32[]{:S(2)}, u32[]{:S(2)}) %collective-permute-start.50) | collective-permute-done | bytes 524320 | tf_op jit(solution)/shard_map/ppermute | solution.py:53
  471.3 6.7 collective-permute-done.51
  487.1 5.8 fusion.133
  503.3 7.5 collective-permute-done.65
  543.8 7.5 collective-permute-done.57
  563.9 9.9 %collective-permute-done.58 = bf16[128,2048]{1,0:T(8,128)(2,1)} collective-permute-done((bf16[128,2048]{1,0:T(8,128)(2,1)S(1)}, bf16[128,2048]{1,0:T(8,128)(2,1)}, u32[]{:S(2)}, u32[]{:S(2)}) %collective-permute-start.58) | collective-permute-done | bytes 524320 | tf_op jit(solution)/shard_map/ppermute | solution.py:53
  579.2 13.5 %collective-permute-done.59 = bf16[128,2048]{1,0:T(8,128)(2,1)S(1)} collective-permute-done((bf16[128,2048]{1,0:T(8,128)(2,1)}, bf16[128,2048]{1,0:T(8,128)(2,1)S(1)}, u32[]{:S(2)}, u32[]{:S(2)}) %collective-permute-start.59) | collective-permute-done | bytes 524320 | tf_op jit(solution)/shard_map/ppermute | solution.py:53
  600.3 13.7 %attend_back.2 = (bf16[512,768]{1,0:T(8,128)(2,1)S(1)}, bf16[512,768]{1,0:T(8,128)(2,1)S(1)}, f32[8,768]{1,0:T(8,128)S(1)}) custom-call(s32[3]{0:T(128)S(1)} %copy-done.20, bf16[512,256]{1,0:T(8,128)(2,1)S(1)} %convolution_convert_fusion.9.own_ref, bf16[512,256]{1,0:T(8,128)(2,1)S(1)} %convolution_convert_fusion.8.sib_ref, bf16[1024,768]{1,0:T(8,128)(2,1)S(1)} %copy-done.22, ...), custom_call_target="tpu_custom_call" | custom-call | flops 5368709120 | bytes 8388608 | tf_op jit(solution)/shard_map/attend_back/pallas_call | solution.py:326
  616.2 7.0 attend_back.3
  638.6 6.1 add_convert_fusion.4
  681.6 6.2 collective-permute-done.85
  687.7 5.7 collective-permute-start.100
  709.2 5.7 collective-permute-done.86
  715.2 6.4 collective-permute-start.87
  726.8 8.8 %collective-permute-done.87 = bf16[128,2048]{1,0:T(8,128)(2,1)S(1)} collective-permute-done((bf16[128,2048]{1,0:T(8,128)(2,1)S(1)}, bf16[128,2048]{1,0:T(8,128)(2,1)S(1)}, u32[]{:S(2)}, u32[]{:S(2)}) %collective-permute-start.87) | collective-permute-done | bytes 524320 | tf_op jit(solution)/shard_map/ppermute | solution.py:53
  (754 shorter events, 465.4 us)
Async XLA Ops:
  7.2 218.7 %all-gather.14.cloned.1.call-start = ((), (), s32[]{:S(2)}) async-start(), calls=%async_computation.11 | async-start | bytes 4718592 | tf_op jit(solution)/shard_map/all_gather | solution.py:506
  12.6 243.0 %all-gather.12.cloned.1.call-start = ((), (), s32[]{:S(2)}) async-start(), calls=%async_computation.10 | async-start | bytes 3604480 | tf_op jit(solution)/shard_map/all_gather | solution.py:409
  13.4 253.5 %all-gather.10.cloned.1.call-start = ((), (), s32[]{:S(2)}) async-start(), calls=%async_computation.9 | async-start | bytes 4718592 | tf_op jit(solution)/shard_map/all_gather | solution.py:506
  14.1 296.6 %all-gather.8.cloned.1.call-start = ((), (), s32[]{:S(2)}) async-start(), calls=%async_computation.8 | async-start | bytes 3604480 | tf_op jit(solution)/shard_map/all_gather | solution.py:408
  34.1 37.6 %collective-permute-start.8 = (bf16[128,2048]{1,0:T(8,128)(2,1)S(1)}, bf16[128,2048]{1,0:T(8,128)(2,1)}, u32[]{:S(2)}, u32[]{:S(2)}) collective-permute-start(bf16[128,2048]{1,0:T(8,128)(2,1)S(1)} %get-tuple-element.231), channel_id=1, source_target_pairs={{2,0},{3,1},{4,2},{5,3},{6,4},{7,5},{10,8},{11,9},{12,10},{13,11},... | collective-permute-start | bytes 1572872 | tf_op jit(solution)/shard_map/ppermute | solution.py:53
  35.4 37.6 %collective-permute-start.7 = (bf16[128,2048]{1,0:T(8,128)(2,1)S(1)}, bf16[128,2048]{1,0:T(8,128)(2,1)}, u32[]{:S(2)}, u32[]{:S(2)}) collective-permute-start(bf16[128,2048]{1,0:T(8,128)(2,1)S(1)} %get-tuple-element.231), channel_id=1, source_target_pairs={{0,2},{1,3},{2,4},{3,5},{4,6},{5,7},{8,10},{9,11},{10,12},{11,13},... | collective-permute-start | bytes 1572872 | tf_op jit(solution)/shard_map/ppermute | solution.py:53
  40.8 275.1 %all-gather.6.cloned.1.call-start = ((), (), s32[]{:S(2)}) async-start(), calls=%async_computation.7 | async-start | bytes 3604480 | tf_op jit(solution)/shard_map/all_gather | solution.py:407
  40.9 42.0 %collective-permute-start.22 = (bf16[128,2048]{1,0:T(8,128)(2,1)S(1)}, bf16[128,2048]{1,0:T(8,128)(2,1)}, u32[]{:S(2)}, u32[]{:S(2)}) collective-permute-start(bf16[128,2048]{1,0:T(8,128)(2,1)S(1)} %get-tuple-element.232), channel_id=1, source_target_pairs={{2,0},{3,1},{4,2},{5,3},{6,4},{7,5},{10,8},{11,9},{12,10},{13,11},... | collective-permute-start | bytes 1572872 | tf_op jit(solution)/shard_map/ppermute | solution.py:53
  42.2 42.0 %collective-permute-start.21 = (bf16[128,2048]{1,0:T(8,128)(2,1)S(1)}, bf16[128,2048]{1,0:T(8,128)(2,1)}, u32[]{:S(2)}, u32[]{:S(2)}) collective-permute-start(bf16[128,2048]{1,0:T(8,128)(2,1)S(1)} %get-tuple-element.232), channel_id=1, source_target_pairs={{0,2},{1,3},{2,4},{3,5},{4,6},{5,7},{8,10},{9,11},{10,12},{11,13},... | collective-permute-start | bytes 1572872 | tf_op jit(solution)/shard_map/ppermute | solution.py:53
  157.6 25.5 %collective-permute-start.15 = (bf16[128,2048]{1,0:T(8,128)(2,1)S(1)}, bf16[128,2048]{1,0:T(8,128)(2,1)S(1)}, u32[]{:S(2)}, u32[]{:S(2)}) collective-permute-start(bf16[128,2048]{1,0:T(8,128)(2,1)S(1)} %get-tuple-element.220), channel_id=1, source_target_pairs={{0,2},{1,3},{8,10},{9,11},{16,18},{17,19},{24,26},{25,27}} | collective-permute-start | bytes 1572872 | tf_op jit(solution)/shard_map/ppermute | solution.py:53
  161.8 32.5 %collective-permute-start.35 = (bf16[128,2048]{1,0:T(8,128)(2,1)S(1)}, bf16[128,2048]{1,0:T(8,128)(2,1)S(1)}, u32[]{:S(2)}, u32[]{:S(2)}) collective-permute-start(bf16[128,2048]{1,0:T(8,128)(2,1)S(1)} %get-tuple-element.226), channel_id=1, source_target_pairs={{0,2},{1,3},{8,10},{9,11},{16,18},{17,19},{24,26},{25,27}} | collective-permute-start | bytes 1572872 | tf_op jit(solution)/shard_map/ppermute | solution.py:53
  164.4 29.9 %collective-permute-start.38 = (bf16[128,2048]{1,0:T(8,128)(2,1)S(1)}, bf16[128,2048]{1,0:T(8,128)(2,1)S(1)}, u32[]{:S(2)}, u32[]{:S(2)}) collective-permute-start(bf16[128,2048]{1,0:T(8,128)(2,1)S(1)} %get-tuple-element.227), channel_id=1, source_target_pairs={{6,4},{7,5},{14,12},{15,13},{22,20},{23,21},{30,28},{31,29}} | collective-permute-start | bytes 1572872 | tf_op jit(solution)/shard_map/ppermute | solution.py:53
  202.1 313.3 %reduce-scatter.8.cloned.1.call-start = ((), (), s32[]{:S(2)}) async-start(), calls=%async_computation.12 | async-start | bytes 4718592 | tf_op jit(solution)/shard_map/reduce_scatter | solution.py:487
  300.5 32.7 %collective-permute-start.47 = (bf16[512,2048]{1,0:T(8,128)(2,1)}, bf16[512,2048]{1,0:T(8,128)(2,1)}, u32[]{:S(2)}, u32[]{:S(2)}) collective-permute-start(bf16[512,2048]{1,0:T(8,128)(2,1)} %pad_maximum_fusion.3), channel_id=1, source_target_pairs={{0,1},{1,0},{2,3},{3,2},{4,5},{5,4},{6,7},{7,6},{8,9},{9,8},{10,11... | collective-permute-start | bytes 6291464 | tf_op jit(solution)/shard_map/ppermute | solution.py:57
  348.1 171.4 %reduce-scatter.10.cloned.1.call-start = ((), (), s32[]{:S(2)}) async-start(), calls=%async_computation.13 | async-start | bytes 4718592 | tf_op jit(solution)/shard_map/reduce_scatter | solution.py:487
  365.8 264.3 %reduce-scatter.20.cloned.1.call-start = ((), (), s32[]{:S(2)}) async-start(), calls=%async_computation.18 | async-start | bytes 3604480 | tf_op jit(solution)/shard_map/reduce_scatter | solution.py:533
  400.1 232.4 %reduce-scatter.16.cloned.1.call-start = ((), (), s32[]{:S(2)}) async-start(), calls=%async_computation.16 | async-start | bytes 3604480 | tf_op jit(solution)/shard_map/reduce_scatter | solution.py:533
  402.5 59.8 %collective-permute-start.63 = (bf16[128,2048]{1,0:T(8,128)(2,1)}, bf16[128,2048]{1,0:T(8,128)(2,1)}, u32[]{:S(2)}, u32[]{:S(2)}) collective-permute-start(bf16[128,2048]{1,0:T(8,128)(2,1)} %get-tuple-element.214), channel_id=1, source_target_pairs={{0,2},{1,3},{8,10},{9,11},{16,18},{17,19},{24,26},{25,27}} | collective-permute-start | bytes 1572872 | tf_op jit(solution)/shard_map/ppermute | solution.py:53
  405.6 56.7 %collective-permute-start.66 = (bf16[128,2048]{1,0:T(8,128)(2,1)}, bf16[128,2048]{1,0:T(8,128)(2,1)}, u32[]{:S(2)}, u32[]{:S(2)}) collective-permute-start(bf16[128,2048]{1,0:T(8,128)(2,1)} %get-tuple-element.215), channel_id=1, source_target_pairs={{6,4},{7,5},{14,12},{15,13},{22,20},{23,21},{30,28},{31,29}} | collective-permute-start | bytes 1572872 | tf_op jit(solution)/shard_map/ppermute | solution.py:53
  412.8 37.8 %collective-permute-start.50 = (bf16[128,2048]{1,0:T(8,128)(2,1)S(1)}, bf16[128,2048]{1,0:T(8,128)(2,1)S(1)}, u32[]{:S(2)}, u32[]{:S(2)}) collective-permute-start(bf16[128,2048]{1,0:T(8,128)(2,1)S(1)} %get-tuple-element.208), channel_id=1, source_target_pairs={{0,2},{1,3},{8,10},{9,11},{16,18},{17,19},{24,26},{25,27}} | collective-permute-start | bytes 1572872 | tf_op jit(solution)/shard_map/ppermute | solution.py:53
  414.2 36.3 %collective-permute-start.53 = (bf16[128,2048]{1,0:T(8,128)(2,1)S(1)}, bf16[128,2048]{1,0:T(8,128)(2,1)S(1)}, u32[]{:S(2)}, u32[]{:S(2)}) collective-permute-start(bf16[128,2048]{1,0:T(8,128)(2,1)S(1)} %get-tuple-element.209), channel_id=1, source_target_pairs={{6,4},{7,5},{14,12},{15,13},{22,20},{23,21},{30,28},{31,29}} | collective-permute-start | bytes 1572872 | tf_op jit(solution)/shard_map/ppermute | solution.py:53
  451.9 26.1 %collective-permute-start.51 = (bf16[128,2048]{1,0:T(8,128)(2,1)}, bf16[128,2048]{1,0:T(8,128)(2,1)}, u32[]{:S(2)}, u32[]{:S(2)}) collective-permute-start(bf16[128,2048]{1,0:T(8,128)(2,1)} %get-tuple-element.206), channel_id=1, source_target_pairs={{0,2},{1,3},{2,4},{3,5},{8,10},{9,11},{10,12},{11,13},{16,18},{17,... | collective-permute-start | bytes 1572872 | tf_op jit(solution)/shard_map/ppermute | solution.py:53
  465.1 27.8 %collective-permute-start.64 = (bf16[128,2048]{1,0:T(8,128)(2,1)}, bf16[128,2048]{1,0:T(8,128)(2,1)}, u32[]{:S(2)}, u32[]{:S(2)}) collective-permute-start(bf16[128,2048]{1,0:T(8,128)(2,1)} %get-tuple-element.212), channel_id=1, source_target_pairs={{0,2},{1,3},{2,4},{3,5},{8,10},{9,11},{10,12},{11,13},{16,18},{17,... | collective-permute-start | bytes 1572872 | tf_op jit(solution)/shard_map/ppermute | solution.py:53
  492.9 142.1 %reduce-scatter.18.cloned.1.call-start = ((), (), s32[]{:S(2)}) async-start(), calls=%async_computation.17 | async-start | bytes 3604480 | tf_op jit(solution)/shard_map/reduce_scatter | solution.py:533
  542.3 33.0 %collective-permute-start.81 = (bf16[128,2048]{1,0:T(8,128)(2,1)S(1)}, bf16[128,2048]{1,0:T(8,128)(2,1)}, u32[]{:S(2)}, u32[]{:S(2)}) collective-permute-start(bf16[128,2048]{1,0:T(8,128)(2,1)S(1)} %collective-permute-done.77), channel_id=1, source_target_pairs={{2,4},{3,5},{4,6},{5,7},{10,12},{11,13},{12,14},{13,15},{18,20},{1... | collective-permute-start | bytes 1572872 | tf_op jit(solution)/shard_map/ppermute | solution.py:53
  552.6 24.7 %collective-permute-start.60 = (bf16[128,2048]{1,0:T(8,128)(2,1)}, bf16[128,2048]{1,0:T(8,128)(2,1)}, u32[]{:S(2)}, u32[]{:S(2)}) collective-permute-start(bf16[128,2048]{1,0:T(8,128)(2,1)} %collective-permute-done.56), channel_id=1, source_target_pairs={{2,4},{3,5},{4,6},{5,7},{10,12},{11,13},{12,14},{13,15},{18,20},{1... | collective-permute-start | bytes 1572872 | tf_op jit(solution)/shard_map/ppermute | solution.py:53
  557.5 199.9 %reduce-scatter.14.cloned.1.call-start = ((), (), s32[]{:S(2)}) async-start(), calls=%async_computation.15 | async-start | bytes 1310720 | tf_op jit(solution)/shard_map/reduce_scatter | solution.py:533
  562.7 32.0 %collective-permute-start.80 = (bf16[128,2048]{1,0:T(8,128)(2,1)}, bf16[128,2048]{1,0:T(8,128)(2,1)S(1)}, u32[]{:S(2)}, u32[]{:S(2)}) collective-permute-start(bf16[128,2048]{1,0:T(8,128)(2,1)} %collective-permute-done.79), channel_id=1, source_target_pairs={{2,0},{3,1},{10,8},{11,9},{18,16},{19,17},{26,24},{27,25}} | collective-permute-start | bytes 1572872 | tf_op jit(solution)/shard_map/ppermute | solution.py:53
  649.4 26.8 %collective-permute-start.71 = (bf16[128,2048]{1,0:T(8,128)(2,1)}, bf16[128,2048]{1,0:T(8,128)(2,1)}, u32[]{:S(2)}, u32[]{:S(2)}) collective-permute-start(bf16[128,2048]{1,0:T(8,128)(2,1)} %get-tuple-element.196), channel_id=1, source_target_pairs={{0,2},{1,3},{8,10},{9,11},{16,18},{17,19},{24,26},{25,27}} | collective-permute-start | bytes 1572872 | tf_op jit(solution)/shard_map/ppermute | solution.py:53
  660.5 98.7 %reduce-scatter.12.cloned.1.call-start = ((), (), s32[]{:S(2)}) async-start(), calls=%async_computation.14 | async-start | bytes 3932160 | tf_op jit(solution)/shard_map/reduce_scatter | solution.py:533
  679.1 23.5 %collective-permute-start.75 = (bf16[128,2048]{1,0:T(8,128)(2,1)S(1)}, bf16[128,2048]{1,0:T(8,128)(2,1)S(1)}, u32[]{:S(2)}, u32[]{:S(2)}) collective-permute-start(bf16[128,2048]{1,0:T(8,128)(2,1)S(1)} %get-tuple-element.195), channel_id=1, source_target_pairs={{4,2},{5,3},{6,4},{7,5},{12,10},{13,11},{14,12},{15,13},{20,18},{2... | collective-permute-start | bytes 1572872 | tf_op jit(solution)/shard_map/ppermute | solution.py:53
  679.9 23.8 %collective-permute-start.98 = (f32[12,16]{1,0:T(8,128)S(1)}, f32[12,16]{1,0:T(8,128)S(1)}, u32[]{:S(2)}, u32[]{:S(2)}) collective-permute-start(f32[12,16]{1,0:T(8,128)S(1)} %get-tuple-element.245), channel_id=1, source_target_pairs={{0,8},{8,16},{16,24},{24,0},{1,9},{9,17},{17,25},{25,1},{2,10},{10... | collective-permute-start | bytes 2312 | tf_op jit(solution)/shard_map/ppermute | solution.py:121
  (244 other events, 3045.3 us)
Sparse Core Ops, SparseCore 0:
  12.7 64.0 all-gather.13
  78.6 48.5 all-gather.11
  129.4 53.1 all-gather.9
  184.3 45.6 all-gather.7
  231.7 41.6 all-gather.5
  348.2 49.6 reduce-scatter.7
  400.1 78.4 reduce-scatter.9
  481.7 42.3 reduce-scatter.19
  527.1 41.7 reduce-scatter.15
  571.8 41.7 reduce-scatter.17
  660.6 32.2 reduce-scatter.13
  696.1 43.9 reduce-scatter.11
